TPU v7x, 32 devices: a whole 2x2x4 slice. The times are simulated.
32 devices in a mesh: grp: 2 (over x), wide: 16 (over z, y, core).
Axes of the slice: x: 2, y: 2, z: 4, core: 2. Of those that a mesh axis runs over, the one named last changes fastest.
Arguments:
- query_rows: bfloat16 [2048, 2048], P(('grp', 'wide')), parts along dimension 0, may hold values from -10 to 10
- row_key_value: bfloat16 [2048, 512], P(('grp', 'wide')), parts along dimension 0, may hold values from -6 to 6
- key_value_cache: bfloat16 [65536, 512], P(('grp', 'wide')), parts along dimension 0, may hold values from -5 to 5
- resid: bfloat16 [2048, 2048], P(('grp', 'wide')), parts along dimension 0, may hold values from -12 to 12
- norm_gain: float32 [2048], replicated, may hold values from 0.5 to 1.5
- lengths: int32 [16], P('grp'), parts along dimension 0, may hold values from 1024 to 4096, as said below
- positions: int32 [16, 128], P('grp'), parts along dimension 0, may hold values from 0 to 4095, as said below
- expert_ids: int32 [2048, 8], P(('grp', 'wide')), parts along dimension 0, may hold values from 0 to 15, all different within a row; in each aligned block of 64 rows (0 to 63, 64 to 127, ...) at most 48 rows name the same one
- gate_scores: float32 [2048, 8], P(('grp', 'wide')), parts along dimension 0, may hold values from 0.1 to 1
- w_gate: bfloat16 [16, 2048, 768], P('wide'), may hold values from -0.125 to 0.125
- w_up: bfloat16 [16, 2048, 768], P('wide'), may hold values from -0.125 to 0.125
- w_down: bfloat16 [16, 768, 2048], P('wide'), may hold values from -0.21875 to 0.21875
Outputs:
- out_rows: bfloat16 [2048, 2048], P(('grp', 'wide')), parts along dimension 0
There are 2 independent parts, one for each index of `grp`. A program takes and returns all parts, laid end to end along the dimension named above; an argument that names none is the same for every part. Nothing has to cross between parts.
Inputs may be any that keep to these rules, and one draw needn't show every extreme that they name: `lengths`: one document has length exactly 4096 and another exactly 1024. Within a document the positions are distinct and below its length. `expert_ids`: the 64 rows of one device name each expert at most 48 times, and some expert exactly that often.
All inputs are finite; a program needn't handle non-finite values.
Results may differ from a plain program's by a relative error of at most 0.0095.
Values may be sent and summed in bfloat16 or wider, within the bound.
No kernel may reach another device: no remote copies, remote signals or barrier semaphores. Data moves between devices by JAX's collectives and lax.ppermute only.
A program may use at most 128 MiB of HBM per device.

v0:
```python
import functools
import math

import jax
import jax.numpy as jnp
from jax import lax
from jax.experimental import pallas as pl
from jax.experimental.pallas import tpu as pltpu
from jax.sharding import PartitionSpec as P


QUERY_HEADS = 32
KEY_VALUE_HEADS = 4
HEAD_SIZE = 64


score_masked_rows = -1e30


def exchanged(shard, axis, distance):
    return lax.ppermute(shard, axis, [(i, i ^ distance) for i in range(lax.axis_size(axis))])


LANES = 128


def cache_kernel(
    device_ref, lengths_ref, positions_ref, own_ref, visit_ref, row_k_ref, row_v_ref, cache_k_ref, cache_v_ref,
    own_out_ref, own_stats_ref, visit_out_ref,
    closed, keys, values, stacked, result, shifts, stats,
):
    group = pl.program_id(0)
    rows = own_ref.shape[0]
    span = cache_k_ref.shape[0]
    pairs = own_ref.shape[1] // LANES
    key_count = keys.shape[0]
    padded = key_count - span
    lane = lax.broadcasted_iota(jnp.int32, (1, LANES), 1)
    low = lane < HEAD_SIZE

    @pl.when(group == 0)
    def _():
        device = device_ref[0]
        start = (device % 2) * span
        length = lengths_ref[device // 2]
        marked = positions_ref[pl.ds(device // 2, 1), :]
        counter = jnp.ones((marked.shape[1], LANES), jnp.bfloat16)
        step = LANES

        def mark(block, carry):
            location = start + block * step + lax.broadcasted_iota(jnp.int32, (step, 1), 0)
            equal = jnp.where(location == marked, 1.0, 0.0).astype(jnp.bfloat16)
            count = jnp.dot(equal, counter, preferred_element_type=jnp.float32)
            shut = ((count > 0.5) | (location >= length)) & (lane == HEAD_SIZE)
            at = pl.ds(pl.multiple_of(block * step, step), step)
            closed[at, :] = jnp.where(shut, score_masked_rows, 0.0).astype(jnp.bfloat16)
            return carry

        lax.fori_loop(0, span // step, mark, 0)
        beyond = lax.broadcasted_iota(jnp.int32, (padded, 1), 0) >= rows
        closed[span:, :] = jnp.where(beyond & (lane == HEAD_SIZE), score_masked_rows, 0.0).astype(jnp.bfloat16)
        stats[...] = jnp.zeros_like(stats)
        if padded > rows:
            keys[span + rows :, :] = closed[span + rows :, :]
            values[span + rows :, :] = jnp.zeros((padded - rows, LANES), jnp.bfloat16)

    first = group % 2 == 0
    zero = jnp.bfloat16(0.0)
    one = jnp.bfloat16(1.0)

    def placed(block, rest):
        wide = block.astype(jnp.float32)
        moved = jnp.where(first, wide, pltpu.roll(wide, HEAD_SIZE, 1)).astype(jnp.bfloat16)
        return jnp.where(low, moved, rest)

    keys[:span, :] = placed(cache_k_ref[...], closed[:span, :])
    values[:span, :] = placed(cache_v_ref[...], one)
    keys[span : span + rows, :] = placed(row_k_ref[...], zero)
    values[span : span + rows, :] = placed(row_v_ref[...], one)
    scale = 1.0 / math.sqrt(HEAD_SIZE)
    marker = jnp.where(lane == HEAD_SIZE, 1.0, 0.0)
    for pair in range(pairs):
        for source, ref in enumerate((own_ref, visit_ref)):
            query = ref[:, pair * LANES : (pair + 1) * LANES].astype(jnp.float32) * scale
            for parity in range(2):
                base = ((parity * pairs + pair) * 2 + source) * rows
                moved = query if parity == 0 else pltpu.roll(query, HEAD_SIZE, 1)
                stacked[base : base + rows, :] = jnp.where(low, moved, marker).astype(jnp.bfloat16)

    chunk = 4 * rows
    for begin in range(0, stacked.shape[0], chunk):
        at = slice(begin, begin + chunk)
        scores = lax.dot_general(
            stacked[at, :], keys[...], (((1,), (1,)), ((), ())), preferred_element_type=jnp.float32
        )
        shift = jnp.max(scores, axis=1, keepdims=True).astype(jnp.bfloat16).astype(jnp.float32)
        weights = jnp.exp(scores - shift).astype(jnp.bfloat16)
        result[at, :] = jnp.dot(weights, values[...], preferred_element_type=jnp.float32)
        shifts[at, :] = jnp.broadcast_to(shift, (chunk, LANES))

    both = 2 * rows
    seen = stats[...]
    for pair in range(pairs):
        even = slice(pair * both, (pair + 1) * both)
        odd = slice((pairs + pair) * both, (pairs + pair + 1) * both)
        joined = jnp.where(low, result[even, :], pltpu.roll(result[odd, :], HEAD_SIZE, 1))
        own_out_ref[:, pair * LANES : (pair + 1) * LANES] = joined[:rows]
        column = pl.multiple_of((group * pairs + pair) * LANES, LANES)
        visit_out_ref[:, pl.ds(column, LANES)] = joined[rows:].astype(jnp.bfloat16)
        for parity, at in enumerate((even, odd)):
            head = (group * pairs + pair) * 2 + parity
            total = result[at, :]
            high = total.astype(jnp.bfloat16).astype(jnp.float32)
            seen = jnp.where(lane == head, shifts[at, :], seen)
            seen = jnp.where(lane == head + 2 * QUERY_HEADS, high, seen)
            seen = jnp.where(lane == head + 3 * QUERY_HEADS, total - high, seen)
    stats[...] = seen

    @pl.when(group == pl.num_programs(0) - 1)
    def _():
        own_stats_ref[...] = stats[:rows].astype(jnp.bfloat16)
        visit_out_ref[:, visit_out_ref.shape[1] - LANES :] = stats[rows:].astype(jnp.bfloat16)


def attend_cache(device, lengths, positions, own, visit, row_key_value, key_value_cache):
    rows, width = own.shape
    span = key_value_cache.shape[0]
    key_count = span + -(-rows // LANES) * LANES
    group_width = width // KEY_VALUE_HEADS
    stack = 2 * rows * (QUERY_HEADS // KEY_VALUE_HEADS)
    half = KEY_VALUE_HEADS * HEAD_SIZE // LANES
    per_block = LANES // HEAD_SIZE
    in_hbm = functools.partial(pltpu.with_memory_space_constraint, memory_space=pltpu.HBM)
    own, row_key_value, key_value_cache, positions = map(in_hbm, (own, row_key_value, key_value_cache, positions))
    return pl.pallas_call(
        cache_kernel,
        grid=(KEY_VALUE_HEADS,),
        in_specs=[
            pl.BlockSpec(memory_space=pltpu.SMEM),
            pl.BlockSpec(memory_space=pltpu.SMEM),
            pl.BlockSpec(positions.shape, lambda g: (0, 0)),
            pl.BlockSpec((rows, group_width), lambda g: (0, g)),
            pl.BlockSpec((rows, group_width), lambda g: (0, g)),
            pl.BlockSpec((rows, LANES), lambda g: (0, g // per_block)),
            pl.BlockSpec((rows, LANES), lambda g: (0, half + g // per_block)),
            pl.BlockSpec((span, LANES), lambda g: (0, g // per_block)),
            pl.BlockSpec((span, LANES), lambda g: (0, half + g // per_block)),
        ],
        out_specs=[
            pl.BlockSpec((rows, group_width), lambda g: (0, g)),
            pl.BlockSpec((rows, LANES), lambda g: (0, 0)),
            pl.BlockSpec((rows, width + LANES), lambda g: (0, 0)),
        ],
        out_shape=[
            jax.ShapeDtypeStruct((rows, width), jnp.float32),
            jax.ShapeDtypeStruct((rows, LANES), jnp.bfloat16),
            jax.ShapeDtypeStruct((rows, width + LANES), jnp.bfloat16),
        ],
        scratch_shapes=[
            pltpu.VMEM((key_count, LANES), jnp.bfloat16),
            pltpu.VMEM((key_count, LANES), jnp.bfloat16),
            pltpu.VMEM((key_count, LANES), jnp.bfloat16),
            pltpu.VMEM((stack, LANES), jnp.bfloat16),
            pltpu.VMEM((stack, LANES), jnp.float32),
            pltpu.VMEM((stack, LANES), jnp.float32),
            pltpu.VMEM((2 * rows, LANES), jnp.float32),
        ],
        compiler_params=pltpu.CompilerParams(vmem_limit_bytes=20 << 20),
        name="cache_attention",
    )(
        device.reshape(1), lengths, positions, own, visit,
        row_key_value, row_key_value, key_value_cache, key_value_cache,
    )


def merge_kernel(own_ref, own_stats_ref, far_ref, resid_ref, gain_ref, shares_ref, payload_ref, residual_ref):
    width = own_ref.shape[1]
    far_stats = far_ref[:, width:]
    head_of = lax.broadcasted_iota(jnp.int32, (LANES, width), 1) // HEAD_SIZE
    stat = lax.broadcasted_iota(jnp.int32, (LANES, width), 0)

    def spread(stats):
        pick_shift = jnp.where(stat == head_of, 1.0, 0.0).astype(jnp.bfloat16)
        pick_total = jnp.where(
            (stat == head_of + 2 * QUERY_HEADS) | (stat == head_of + 3 * QUERY_HEADS), 1.0, 0.0
        ).astype(jnp.bfloat16)
        return (
            jnp.dot(stats, pick_shift, preferred_element_type=jnp.float32),
            jnp.dot(stats, pick_total, preferred_element_type=jnp.float32),
        )

    own_shift, own_total = spread(own_stats_ref[...])
    far_shift, far_total = spread(far_stats)
    joint = jnp.maximum(own_shift, far_shift)
    own_scale = jnp.exp(own_shift - joint)
    far_scale = jnp.exp(far_shift - joint)
    merged = own_ref[...] * own_scale + far_ref[:, :width].astype(jnp.float32) * far_scale
    total = own_total * own_scale + far_total * far_scale
    attn = (merged / total).astype(jnp.bfloat16).astype(jnp.float32)
    residual = resid_ref[...].astype(jnp.float32) + attn
    residual_ref[...] = residual
    power = jnp.mean(residual * residual, axis=1, keepdims=True)
    normed = residual * lax.rsqrt(power + 1e-06) * gain_ref[...]
    payload_ref[:, :width] = normed.astype(jnp.bfloat16)
    payload_ref[:, width:] = shares_ref[...]


def merge(own, own_stats, far, resid, norm_gain, shares):
    rows, width = own.shape
    return pl.pallas_call(
        merge_kernel,
        out_shape=[
            jax.ShapeDtypeStruct((rows, width + shares.shape[1]), jnp.bfloat16),
            jax.ShapeDtypeStruct((rows, width), jnp.float32),
        ],
        compiler_params=pltpu.CompilerParams(vmem_limit_bytes=12 << 20),
        name="merge_norm",
    )(own, own_stats, far, resid, norm_gain.reshape(1, width), shares)


def expert_kernel(device_ref, near_ref, far_ref, gate_ref, up_ref, down_ref, keep_ref, send_ref, *, experts):
    depth = gate_ref.shape[1]
    hidden_width = gate_ref.shape[2]
    rows = jnp.concatenate([near_ref[...], far_ref[...]], axis=0)
    device = device_ref[0]
    column = lax.broadcasted_iota(jnp.int32, (1, rows.shape[1] - depth), 1)
    own_column = (column == device) | (column == device + experts)
    share = jnp.sum(
        jnp.where(own_column, rows[:, depth:].astype(jnp.float32), 0.0), axis=1, keepdims=True
    )
    rows = rows[:, :depth]
    step = 256
    hidden = []
    for begin in range(0, hidden_width, step):
        at = slice(begin, min(begin + step, hidden_width))
        gate_act = jnp.dot(rows, gate_ref[0, :, at], preferred_element_type=jnp.float32)
        up_act = jnp.dot(rows, up_ref[0, :, at], preferred_element_type=jnp.float32)
        hidden.append((jax.nn.silu(gate_act) * up_act).astype(jnp.bfloat16))
    hidden = jnp.concatenate(hidden, axis=1)
    kept = keep_ref.shape[0]
    step = 512
    for begin in range(0, depth, step):
        at = slice(begin, min(begin + step, depth))
        expert_out = jnp.dot(hidden, down_ref[0, :, at], preferred_element_type=jnp.float32)
        partial = share * expert_out.astype(jnp.bfloat16).astype(jnp.float32)
        keep_ref[:, at] = partial[:kept]
        send_ref[:, at] = partial[kept:].astype(jnp.bfloat16)


def expert(device, near, far, w_gate, w_up, w_down, experts):
    rows = near.shape[0]
    depth = w_gate.shape[1]
    return pl.pallas_call(
        functools.partial(expert_kernel, experts=experts),
        in_specs=[pl.BlockSpec(memory_space=pltpu.SMEM)] + [pl.BlockSpec(memory_space=pltpu.VMEM)] * 5,
        out_specs=[pl.BlockSpec(memory_space=pltpu.VMEM)] * 2,
        out_shape=[
            jax.ShapeDtypeStruct((rows, depth), jnp.float32),
            jax.ShapeDtypeStruct((rows, depth), jnp.bfloat16),
        ],
        compiler_params=pltpu.CompilerParams(vmem_limit_bytes=20 << 20),
        name="expert",
    )(device.reshape(1), near, far, w_gate, w_up, w_down)


def local(
    query_rows,
    row_key_value,
    key_value_cache,
    resid,
    norm_gain,
    lengths,
    positions,
    expert_ids,
    gate_scores,
    w_gate,
    w_up,
    w_down,
):
    masked_row_count, _ = resid.shape
    device = lax.axis_index("wide")
    experts = lax.axis_size("wide")
    mix = gate_scores / jnp.sum(gate_scores, axis=-1, keepdims=True)
    shares = jnp.sum(
        jnp.where(expert_ids[..., None] == jnp.arange(experts, dtype=jnp.int32), mix[..., None], 0.0), axis=1
    )
    shares_high = shares.astype(jnp.bfloat16)
    shares_low = (shares - shares_high.astype(jnp.float32)).astype(jnp.bfloat16)
    tail = -(-2 * experts // LANES) * LANES
    filler = jnp.zeros((masked_row_count, tail - 2 * experts), jnp.bfloat16)
    shares = jnp.concatenate([shares_high, shares_low, filler], axis=1)
    visitor = exchanged(query_rows, "wide", 1)
    own, own_stats, hosted = attend_cache(
        device, lengths, positions, query_rows, visitor, row_key_value, key_value_cache
    )
    far = exchanged(hosted, "wide", 1)
    payload, residual = merge(own, own_stats, far, resid, norm_gain, shares)
    planes = experts // 4
    blocks = [payload]
    total = residual
    beside, near, far = [], [None] * planes, [None] * planes
    for k in range(1, planes):
        low_bit = k & -k
        blocks.append(exchanged(blocks[k - low_bit], "wide", 4 * low_bit))
    for k in range(planes):
        low_bit = k & -k
        if k > low_bit:
            beside.append(exchanged(beside[k - low_bit], "wide", 4 * low_bit))
        else:
            beside.append(exchanged(blocks[k], "wide", 2))
        near[k] = jnp.concatenate([blocks[k], beside[k]], axis=0)
        far[k] = exchanged(near[k], "wide", 1)
    for k in range(planes):
        kept, sent = expert(device, near[k], far[k], w_gate, w_up, w_down, experts)
        sent = exchanged(sent, "wide", 1)
        half = kept + sent.astype(jnp.float32)
        mine, other = half[:masked_row_count], half[masked_row_count:].astype(jnp.bfloat16)
        other = exchanged(other, "wide", 2)
        mine = mine + other.astype(jnp.float32)
        if k:
            mine = exchanged(mine.astype(jnp.bfloat16), "wide", 4 * k).astype(jnp.float32)
        total = total + mine
    return total.astype(jnp.bfloat16)


def solution(mesh):
    return jax.shard_map(
        local,
        mesh=mesh,
        in_specs=(
            P(("grp", "wide"), None),
            P(("grp", "wide"), None),
            P(("grp", "wide"), None),
            P(("grp", "wide"), None),
            P(),
            P("grp"),
            P("grp", None),
            P(("grp", "wide"), None),
            P(("grp", "wide"), None),
            P("wide", None, None),
            P("wide", None, None),
            P("wide", None, None),
        ),
        out_specs=P(("grp", "wide"), None),
        check_vma=False,
    )
```

profile of v0, /device:TPU:15, one launch (start us, length us, event | category | flops | bytes accessed | tf_op | source)
XLA Modules:
  0.0 116.2 jit_solution(2786941843681435688)
XLA Ops:
  0.0 0.7 collective-permute-start
  0.7 0.7 reduce_sum.18
  1.4 0.7 broadcast_divide_fusion
  2.1 0.7 select_reduce_fusion
  3.0 0.8 copy-done.5
  3.8 19.7 %cache_attention.1 = (f32[64,2048]{1,0:T(8,128)S(1)}, bf16[64,128]{1,0:T(8,128)(2,1)S(1)}, bf16[64,2176]{1,0:T(8,128)(2,1)S(1)}) custom-call(s32[1]{0:T(128)} %bitcast.device_ref, s32[8]{0:T(128)S(1)} %copy-done.5, s32[8,128]{1,0:T(8,128)} %positions_ref.1, bf16[64,2048]{1,0:T(8,128)(2,1)} %own_ref.1, bf16[64,2048]{1,0:T(8,128)(2,1)S(1)} %collective-permute-done.visit_ref, ...), custom_call_target="tpu_custom_call" | custom-call | tf_op jit(solution)/shard_map/cache_attention/pallas_call | solution.py:135
  23.8 1.4 %collective-permute-done.1.far_ref = bf16[64,2176]{1,0:T(8,128)(2,1)S(1)} collective-permute-done((bf16[64,2176]{1,0:T(8,128)(2,1)S(1)}, bf16[64,2176]{1,0:T(8,128)(2,1)S(1)}, u32[]{:S(2)}, u32[]{:S(2)}) %collective-permute-start.1) | collective-permute-done | bytes 278560 | tf_op jit(solution)/shard_map/ppermute | solution.py:21
  25.2 0.9 copy-done.3
  26.1 0.8 merge_norm.1
  26.9 0.2 collective-permute-start.6
  27.1 2.3 %collective-permute-start.12 = (bf16[64,2176]{1,0:T(8,128)(2,1)S(1)}, bf16[64,2176]{1,0:T(8,128)(2,1)S(1)}, u32[]{:S(2)}, u32[]{:S(2)}) collective-permute-start(bf16[64,2176]{1,0:T(8,128)(2,1)S(1)} %get-tuple-element.22), channel_id=1, source_target_pairs={{0,8},{1,9},{2,10},{3,11},{4,12},{5,13},{6,14},{7,15},{8,0},{9,1},... | collective-permute-start | bytes 835592 | tf_op jit(solution)/shard_map/ppermute | solution.py:21
  29.4 0.2 collective-permute-start.2
  29.7 7.3 %collective-permute-done.2 = bf16[64,2176]{1,0:T(8,128)(2,1)S(1)} collective-permute-done((bf16[64,2176]{1,0:T(8,128)(2,1)S(1)}, bf16[64,2176]{1,0:T(8,128)(2,1)S(1)}, u32[]{:S(2)}, u32[]{:S(2)}) %collective-permute-start.2) | collective-permute-done | bytes 278560 | tf_op jit(solution)/shard_map/ppermute | solution.py:21
  37.0 1.6 %collective-permute-start.3 = (bf16[128,2176]{1,0:T(8,128)(2,1)S(1)}, bf16[128,2176]{1,0:T(8,128)(2,1)S(1)}, u32[]{:S(2)}, u32[]{:S(2)}) collective-permute-start(bf16[128,2176]{1,0:T(8,128)(2,1)S(1)} %constant_dynamic-update-slice_fusion.near_ref), channel_id=1, source_target_pairs={{0,1},{1,0},{2,3},{3,2},{4,5},{5,4},{6,7},{7,6},{8,9},{9,8},{10,11... | collective-permute-start | bytes 1671176 | tf_op jit(solution)/shard_map/ppermute | solution.py:21
  38.6 0.3 collective-permute-done.6
  38.9 0.2 collective-permute-start.7
  39.1 3.0 %collective-permute-done.12 = bf16[64,2176]{1,0:T(8,128)(2,1)S(1)} collective-permute-done((bf16[64,2176]{1,0:T(8,128)(2,1)S(1)}, bf16[64,2176]{1,0:T(8,128)(2,1)S(1)}, u32[]{:S(2)}, u32[]{:S(2)}) %collective-permute-start.12) | collective-permute-done | bytes 278560 | tf_op jit(solution)/shard_map/ppermute | solution.py:21
  42.1 0.2 collective-permute-start.13
  42.3 0.3 collective-permute-start.18
  42.7 3.4 %collective-permute-done.7 = bf16[64,2176]{1,0:T(8,128)(2,1)S(1)} collective-permute-done((bf16[64,2176]{1,0:T(8,128)(2,1)S(1)}, bf16[64,2176]{1,0:T(8,128)(2,1)S(1)}, u32[]{:S(2)}, u32[]{:S(2)}) %collective-permute-start.7) | collective-permute-done | bytes 278560 | tf_op jit(solution)/shard_map/ppermute | solution.py:21
  46.1 3.4 %collective-permute-start.8 = (bf16[128,2176]{1,0:T(8,128)(2,1)S(1)}, bf16[128,2176]{1,0:T(8,128)(2,1)S(1)}, u32[]{:S(2)}, u32[]{:S(2)}) collective-permute-start(bf16[128,2176]{1,0:T(8,128)(2,1)S(1)} %constant_dynamic-update-slice_fusion.2.near_ref), channel_id=1, source_target_pairs={{0,1},{1,0},{2,3},{3,2},{4,5},{5,4},{6,7},{7,6},{8,9},{9,8},{10,11... | collective-permute-start | bytes 1671176 | tf_op jit(solution)/shard_map/ppermute | solution.py:21
  49.5 2.6 %collective-permute-done.13 = bf16[64,2176]{1,0:T(8,128)(2,1)S(1)} collective-permute-done((bf16[64,2176]{1,0:T(8,128)(2,1)S(1)}, bf16[64,2176]{1,0:T(8,128)(2,1)S(1)}, u32[]{:S(2)}, u32[]{:S(2)}) %collective-permute-start.13) | collective-permute-done | bytes 278560 | tf_op jit(solution)/shard_map/ppermute | solution.py:21
  52.1 1.9 %collective-permute-start.14 = (bf16[128,2176]{1,0:T(8,128)(2,1)S(1)}, bf16[128,2176]{1,0:T(8,128)(2,1)S(1)}, u32[]{:S(2)}, u32[]{:S(2)}) collective-permute-start(bf16[128,2176]{1,0:T(8,128)(2,1)S(1)} %constant_dynamic-update-slice_fusion.4.near_ref), channel_id=1, source_target_pairs={{0,1},{1,0},{2,3},{3,2},{4,5},{5,4},{6,7},{7,6},{8,9},{9,8},{10,11... | collective-permute-start | bytes 1671176 | tf_op jit(solution)/shard_map/ppermute | solution.py:21
  54.0 2.2 %collective-permute-start.19 = (bf16[64,2176]{1,0:T(8,128)(2,1)S(1)}, bf16[64,2176]{1,0:T(8,128)(2,1)S(1)}, u32[]{:S(2)}, u32[]{:S(2)}) collective-permute-start(bf16[64,2176]{1,0:T(8,128)(2,1)S(1)} %collective-permute-done.13), channel_id=1, source_target_pairs={{0,4},{1,5},{2,6},{3,7},{4,0},{5,1},{6,2},{7,3},{8,12},{9,13},{10,... | collective-permute-start | bytes 835592 | tf_op jit(solution)/shard_map/ppermute | solution.py:21
  56.2 2.6 %expert.4 = (f32[128,2048]{1,0:T(8,128)S(1)}, bf16[128,2048]{1,0:T(8,128)(2,1)S(1)}) custom-call(s32[1]{0:T(128)} %bitcast.device_ref, bf16[128,2176]{1,0:T(8,128)(2,1)S(1)} %constant_dynamic-update-slice_fusion.near_ref, bf16[128,2176]{1,0:T(8,128)(2,1)S(1)} %collective-permute-done.3.far_ref, bf16[1,2048,768]{2,1,0:T(8,128)(2,1)S(1)} %copy-done, ...), custom_call_target="tpu_custom_call" | custom-call | tf_op jit(solution)/shard_map/expert/pallas_call | solution.py:253
  58.8 0.4 collective-permute-start.4
  59.3 3.9 %collective-permute-done.19 = bf16[64,2176]{1,0:T(8,128)(2,1)S(1)} collective-permute-done((bf16[64,2176]{1,0:T(8,128)(2,1)S(1)}, bf16[64,2176]{1,0:T(8,128)(2,1)S(1)}, u32[]{:S(2)}, u32[]{:S(2)}) %collective-permute-start.19) | collective-permute-done | bytes 278560 | tf_op jit(solution)/shard_map/ppermute | solution.py:21
  63.2 0.7 collective-permute-start.20
  63.9 2.6 %expert.5 = (f32[128,2048]{1,0:T(8,128)S(1)}, bf16[128,2048]{1,0:T(8,128)(2,1)S(1)}) custom-call(s32[1]{0:T(128)} %bitcast.device_ref, bf16[128,2176]{1,0:T(8,128)(2,1)S(1)} %constant_dynamic-update-slice_fusion.2.near_ref, bf16[128,2176]{1,0:T(8,128)(2,1)S(1)} %collective-permute-done.8.far_ref, bf16[1,2048,768]{2,1,0:T(8,128)(2,1)S(1)} %copy-done, ...), custom_call_target="tpu_custom_call" | custom-call | tf_op jit(solution)/shard_map/expert/pallas_call | solution.py:253
  66.6 2.6 %expert.6 = (f32[128,2048]{1,0:T(8,128)S(1)}, bf16[128,2048]{1,0:T(8,128)(2,1)S(1)}) custom-call(s32[1]{0:T(128)} %bitcast.device_ref, bf16[128,2176]{1,0:T(8,128)(2,1)S(1)} %constant_dynamic-update-slice_fusion.4.near_ref, bf16[128,2176]{1,0:T(8,128)(2,1)S(1)} %collective-permute-done.14.far_ref, bf16[1,2048,768]{2,1,0:T(8,128)(2,1)S(1)} %copy-done, ...), custom_call_target="tpu_custom_call" | custom-call | tf_op jit(solution)/shard_map/expert/pallas_call | solution.py:253
  69.2 0.6 collective-permute-start.15
  69.8 0.1 convert_add_fusion.3
  69.9 0.3 collective-permute-start.5
  70.2 2.6 %expert.7 = (f32[128,2048]{1,0:T(8,128)S(1)}, bf16[128,2048]{1,0:T(8,128)(2,1)S(1)}) custom-call(s32[1]{0:T(128)} %bitcast.device_ref, bf16[128,2176]{1,0:T(8,128)(2,1)S(1)} %constant_dynamic-update-slice_fusion.6.near_ref, bf16[128,2176]{1,0:T(8,128)(2,1)S(1)} %collective-permute-done.20.far_ref, bf16[1,2048,768]{2,1,0:T(8,128)(2,1)S(1)} %copy-done, ...), custom_call_target="tpu_custom_call" | custom-call | tf_op jit(solution)/shard_map/expert/pallas_call | solution.py:253
  72.9 0.4 collective-permute-start.21
  73.2 0.1 convert_add_fusion.2
  73.4 1.3 %collective-permute-start.10 = (bf16[64,2048]{1,0:T(8,128)(2,1)S(1)}, bf16[64,2048]{1,0:T(8,128)(2,1)S(1)}, u32[]{:S(2)}, u32[]{:S(2)}) collective-permute-start(bf16[64,2048]{1,0:T(8,128)(2,1)S(1)} %slice.70), channel_id=1, source_target_pairs={{0,2},{1,3},{2,0},{3,1},{4,6},{5,7},{6,4},{7,5},{8,10},{9,11},{10,... | collective-permute-start | bytes 786440 | tf_op jit(solution)/shard_map/ppermute | solution.py:21
  74.8 0.3 collective-permute-start.16
  75.1 8.3 %collective-permute-done.10 = bf16[64,2048]{1,0:T(8,128)(2,1)S(1)} collective-permute-done((bf16[64,2048]{1,0:T(8,128)(2,1)S(1)}, bf16[64,2048]{1,0:T(8,128)(2,1)S(1)}, u32[]{:S(2)}, u32[]{:S(2)}) %collective-permute-start.10) | collective-permute-done | bytes 262176 | tf_op jit(solution)/shard_map/ppermute | solution.py:21
  83.5 1.5 %collective-permute-start.11 = (bf16[64,2048]{1,0:T(8,128)(2,1)S(1)}, bf16[64,2048]{1,0:T(8,128)(2,1)S(1)}, u32[]{:S(2)}, u32[]{:S(2)}) collective-permute-start(bf16[64,2048]{1,0:T(8,128)(2,1)S(1)} %fusion.2), channel_id=1, source_target_pairs={{0,4},{1,5},{2,6},{3,7},{4,0},{5,1},{6,2},{7,3},{8,12},{9,13},{10,... | collective-permute-start | bytes 786440 | tf_op jit(solution)/shard_map/ppermute | solution.py:21
  85.2 0.3 collective-permute-start.22
  85.5 3.6 %collective-permute-done.16 = bf16[64,2048]{1,0:T(8,128)(2,1)S(1)} collective-permute-done((bf16[64,2048]{1,0:T(8,128)(2,1)S(1)}, bf16[64,2048]{1,0:T(8,128)(2,1)S(1)}, u32[]{:S(2)}, u32[]{:S(2)}) %collective-permute-start.16) | collective-permute-done | bytes 262176 | tf_op jit(solution)/shard_map/ppermute | solution.py:21
  89.1 2.5 %collective-permute-start.17 = (bf16[64,2048]{1,0:T(8,128)(2,1)S(1)}, bf16[64,2048]{1,0:T(8,128)(2,1)S(1)}, u32[]{:S(2)}, u32[]{:S(2)}) collective-permute-start(bf16[64,2048]{1,0:T(8,128)(2,1)S(1)} %fusion.1), channel_id=1, source_target_pairs={{0,8},{1,9},{2,10},{3,11},{4,12},{5,13},{6,14},{7,15},{8,0},{9,1},... | collective-permute-start | bytes 786440 | tf_op jit(solution)/shard_map/ppermute | solution.py:21
  91.7 3.0 %collective-permute-done.22 = bf16[64,2048]{1,0:T(8,128)(2,1)S(1)} collective-permute-done((bf16[64,2048]{1,0:T(8,128)(2,1)S(1)}, bf16[64,2048]{1,0:T(8,128)(2,1)S(1)}, u32[]{:S(2)}, u32[]{:S(2)}) %collective-permute-start.22) | collective-permute-done | bytes 262176 | tf_op jit(solution)/shard_map/ppermute | solution.py:21
  94.7 1.4 %collective-permute-start.23 = (bf16[64,2048]{1,0:T(8,128)(2,1)S(1)}, bf16[64,2048]{1,0:T(8,128)(2,1)S(1)}, u32[]{:S(2)}, u32[]{:S(2)}) collective-permute-start(bf16[64,2048]{1,0:T(8,128)(2,1)S(1)} %fusion), channel_id=1, source_target_pairs={{0,12},{1,13},{2,14},{3,15},{4,8},{5,9},{6,10},{7,11},{8,4},{9,5},... | collective-permute-start | bytes 786440 | tf_op jit(solution)/shard_map/ppermute | solution.py:21
  96.1 12.6 %collective-permute-done.17 = bf16[64,2048]{1,0:T(8,128)(2,1)S(1)} collective-permute-done((bf16[64,2048]{1,0:T(8,128)(2,1)S(1)}, bf16[64,2048]{1,0:T(8,128)(2,1)S(1)}, u32[]{:S(2)}, u32[]{:S(2)}) %collective-permute-start.17) | collective-permute-done | bytes 262176 | tf_op jit(solution)/shard_map/ppermute | solution.py:21
  108.7 6.6 %collective-permute-done.23 = bf16[64,2048]{1,0:T(8,128)(2,1)S(1)} collective-permute-done((bf16[64,2048]{1,0:T(8,128)(2,1)S(1)}, bf16[64,2048]{1,0:T(8,128)(2,1)S(1)}, u32[]{:S(2)}, u32[]{:S(2)}) %collective-permute-start.23) | collective-permute-done | bytes 262176 | tf_op jit(solution)/shard_map/ppermute | solution.py:21
  115.3 0.9 fusion.7
  (48 shorter events, 1.2 us)
Async XLA Ops:
  0.0 25.2 %copy-start.4 = (f32[2048]{0:T(1024)S(1)}, f32[2048]{0:T(1024)}, u32[]{:S(2)}) copy-start(f32[2048]{0:T(1024)} %param.16) | copy-start | bytes 24580
  0.0 3.0 %collective-permute-start = (bf16[64,2048]{1,0:T(8,128)(2,1)}, bf16[64,2048]{1,0:T(8,128)(2,1)S(1)}, u32[]{:S(2)}, u32[]{:S(2)}) collective-permute-start(bf16[64,2048]{1,0:T(8,128)(2,1)} %own_ref.1), channel_id=1, source_target_pairs={{0,1},{1,0},{2,3},{3,2},{4,5},{5,4},{6,7},{7,6},{8,9},{9,8},{10,11... | collective-permute-start | bytes 786440 | tf_op jit(solution)/shard_map/ppermute | solution.py:21
  2.9 53.3 %copy-start.2 = (bf16[1,768,2048]{2,1,0:T(8,128)(2,1)S(1)}, bf16[1,768,2048]{2,1,0:T(8,128)(2,1)}, u32[]{:S(2)}) copy-start(bf16[1,768,2048]{2,1,0:T(8,128)(2,1)} %down_ref.7) | copy-start | bytes 9437188
  3.0 0.8 copy-start.5
  3.8 52.4 %copy-start.1 = (bf16[1,2048,768]{2,1,0:T(8,128)(2,1)S(1)}, bf16[1,2048,768]{2,1,0:T(8,128)(2,1)}, u32[]{:S(2)}) copy-start(bf16[1,2048,768]{2,1,0:T(8,128)(2,1)} %up_ref.7) | copy-start | bytes 9437188
  23.5 32.7 %copy-start = (bf16[1,2048,768]{2,1,0:T(8,128)(2,1)S(1)}, bf16[1,2048,768]{2,1,0:T(8,128)(2,1)}, u32[]{:S(2)}) copy-start(bf16[1,2048,768]{2,1,0:T(8,128)(2,1)} %gate_ref.7) | copy-start | bytes 9437188
  23.5 1.6 %collective-permute-start.1 = (bf16[64,2176]{1,0:T(8,128)(2,1)S(1)}, bf16[64,2176]{1,0:T(8,128)(2,1)S(1)}, u32[]{:S(2)}, u32[]{:S(2)}) collective-permute-start(bf16[64,2176]{1,0:T(8,128)(2,1)S(1)} %get-tuple-element.20), channel_id=1, source_target_pairs={{0,1},{1,0},{2,3},{3,2},{4,5},{5,4},{6,7},{7,6},{8,9},{9,8},{10,11... | collective-permute-start | bytes 835592 | tf_op jit(solution)/shard_map/ppermute | solution.py:21
  25.2 1.0 copy-start.3
  26.9 12.0 %collective-permute-start.6 = (bf16[64,2176]{1,0:T(8,128)(2,1)S(1)}, bf16[64,2176]{1,0:T(8,128)(2,1)S(1)}, u32[]{:S(2)}, u32[]{:S(2)}) collective-permute-start(bf16[64,2176]{1,0:T(8,128)(2,1)S(1)} %get-tuple-element.22), channel_id=1, source_target_pairs={{0,4},{1,5},{2,6},{3,7},{4,0},{5,1},{6,2},{7,3},{8,12},{9,13},{10,... | collective-permute-start | bytes 835592 | tf_op jit(solution)/shard_map/ppermute | solution.py:21
  27.1 14.9 %collective-permute-start.12 = (bf16[64,2176]{1,0:T(8,128)(2,1)S(1)}, bf16[64,2176]{1,0:T(8,128)(2,1)S(1)}, u32[]{:S(2)}, u32[]{:S(2)}) collective-permute-start(bf16[64,2176]{1,0:T(8,128)(2,1)S(1)} %get-tuple-element.22), channel_id=1, source_target_pairs={{0,8},{1,9},{2,10},{3,11},{4,12},{5,13},{6,14},{7,15},{8,0},{9,1},... | collective-permute-start | bytes 835592 | tf_op jit(solution)/shard_map/ppermute | solution.py:21
  29.4 7.5 %collective-permute-start.2 = (bf16[64,2176]{1,0:T(8,128)(2,1)S(1)}, bf16[64,2176]{1,0:T(8,128)(2,1)S(1)}, u32[]{:S(2)}, u32[]{:S(2)}) collective-permute-start(bf16[64,2176]{1,0:T(8,128)(2,1)S(1)} %get-tuple-element.22), channel_id=1, source_target_pairs={{0,2},{1,3},{2,0},{3,1},{4,6},{5,7},{6,4},{7,5},{8,10},{9,11},{10,... | collective-permute-start | bytes 835592 | tf_op jit(solution)/shard_map/ppermute | solution.py:21
  37.0 19.2 %collective-permute-start.3 = (bf16[128,2176]{1,0:T(8,128)(2,1)S(1)}, bf16[128,2176]{1,0:T(8,128)(2,1)S(1)}, u32[]{:S(2)}, u32[]{:S(2)}) collective-permute-start(bf16[128,2176]{1,0:T(8,128)(2,1)S(1)} %constant_dynamic-update-slice_fusion.near_ref), channel_id=1, source_target_pairs={{0,1},{1,0},{2,3},{3,2},{4,5},{5,4},{6,7},{7,6},{8,9},{9,8},{10,11... | collective-permute-start | bytes 1671176 | tf_op jit(solution)/shard_map/ppermute | solution.py:21
  38.9 7.2 %collective-permute-start.7 = (bf16[64,2176]{1,0:T(8,128)(2,1)S(1)}, bf16[64,2176]{1,0:T(8,128)(2,1)S(1)}, u32[]{:S(2)}, u32[]{:S(2)}) collective-permute-start(bf16[64,2176]{1,0:T(8,128)(2,1)S(1)} %collective-permute-done.6), channel_id=1, source_target_pairs={{0,2},{1,3},{2,0},{3,1},{4,6},{5,7},{6,4},{7,5},{8,10},{9,11},{10,... | collective-permute-start | bytes 835592 | tf_op jit(solution)/shard_map/ppermute | solution.py:21
  42.1 10.0 %collective-permute-start.13 = (bf16[64,2176]{1,0:T(8,128)(2,1)S(1)}, bf16[64,2176]{1,0:T(8,128)(2,1)S(1)}, u32[]{:S(2)}, u32[]{:S(2)}) collective-permute-start(bf16[64,2176]{1,0:T(8,128)(2,1)S(1)} %collective-permute-done.12), channel_id=1, source_target_pairs={{0,2},{1,3},{2,0},{3,1},{4,6},{5,7},{6,4},{7,5},{8,10},{9,11},{10,... | collective-permute-start | bytes 835592 | tf_op jit(solution)/shard_map/ppermute | solution.py:21
  42.3 17.0 %collective-permute-start.18 = (bf16[64,2176]{1,0:T(8,128)(2,1)S(1)}, bf16[64,2176]{1,0:T(8,128)(2,1)S(1)}, u32[]{:S(2)}, u32[]{:S(2)}) collective-permute-start(bf16[64,2176]{1,0:T(8,128)(2,1)S(1)} %collective-permute-done.12), channel_id=1, source_target_pairs={{0,4},{1,5},{2,6},{3,7},{4,0},{5,1},{6,2},{7,3},{8,12},{9,13},{10,... | collective-permute-start | bytes 835592 | tf_op jit(solution)/shard_map/ppermute | solution.py:21
  46.1 17.8 %collective-permute-start.8 = (bf16[128,2176]{1,0:T(8,128)(2,1)S(1)}, bf16[128,2176]{1,0:T(8,128)(2,1)S(1)}, u32[]{:S(2)}, u32[]{:S(2)}) collective-permute-start(bf16[128,2176]{1,0:T(8,128)(2,1)S(1)} %constant_dynamic-update-slice_fusion.2.near_ref), channel_id=1, source_target_pairs={{0,1},{1,0},{2,3},{3,2},{4,5},{5,4},{6,7},{7,6},{8,9},{9,8},{10,11... | collective-permute-start | bytes 1671176 | tf_op jit(solution)/shard_map/ppermute | solution.py:21
  52.1 14.5 %collective-permute-start.14 = (bf16[128,2176]{1,0:T(8,128)(2,1)S(1)}, bf16[128,2176]{1,0:T(8,128)(2,1)S(1)}, u32[]{:S(2)}, u32[]{:S(2)}) collective-permute-start(bf16[128,2176]{1,0:T(8,128)(2,1)S(1)} %constant_dynamic-update-slice_fusion.4.near_ref), channel_id=1, source_target_pairs={{0,1},{1,0},{2,3},{3,2},{4,5},{5,4},{6,7},{7,6},{8,9},{9,8},{10,11... | collective-permute-start | bytes 1671176 | tf_op jit(solution)/shard_map/ppermute | solution.py:21
  54.0 9.2 %collective-permute-start.19 = (bf16[64,2176]{1,0:T(8,128)(2,1)S(1)}, bf16[64,2176]{1,0:T(8,128)(2,1)S(1)}, u32[]{:S(2)}, u32[]{:S(2)}) collective-permute-start(bf16[64,2176]{1,0:T(8,128)(2,1)S(1)} %collective-permute-done.13), channel_id=1, source_target_pairs={{0,4},{1,5},{2,6},{3,7},{4,0},{5,1},{6,2},{7,3},{8,12},{9,13},{10,... | collective-permute-start | bytes 835592 | tf_op jit(solution)/shard_map/ppermute | solution.py:21
  58.8 10.9 %collective-permute-start.4 = (bf16[128,2048]{1,0:T(8,128)(2,1)S(1)}, bf16[128,2048]{1,0:T(8,128)(2,1)S(1)}, u32[]{:S(2)}, u32[]{:S(2)}) collective-permute-start(bf16[128,2048]{1,0:T(8,128)(2,1)S(1)} %get-tuple-element.24), channel_id=1, source_target_pairs={{0,1},{1,0},{2,3},{3,2},{4,5},{5,4},{6,7},{7,6},{8,9},{9,8},{10,11... | collective-permute-start | bytes 1572872 | tf_op jit(solution)/shard_map/ppermute | solution.py:21
  63.2 7.1 %collective-permute-start.20 = (bf16[128,2176]{1,0:T(8,128)(2,1)S(1)}, bf16[128,2176]{1,0:T(8,128)(2,1)S(1)}, u32[]{:S(2)}, u32[]{:S(2)}) collective-permute-start(bf16[128,2176]{1,0:T(8,128)(2,1)S(1)} %constant_dynamic-update-slice_fusion.6.near_ref), channel_id=1, source_target_pairs={{0,1},{1,0},{2,3},{3,2},{4,5},{5,4},{6,7},{7,6},{8,9},{9,8},{10,11... | collective-permute-start | bytes 1671176 | tf_op jit(solution)/shard_map/ppermute | solution.py:21
  66.5 6.7 %collective-permute-start.9 = (bf16[128,2048]{1,0:T(8,128)(2,1)S(1)}, bf16[128,2048]{1,0:T(8,128)(2,1)S(1)}, u32[]{:S(2)}, u32[]{:S(2)}) collective-permute-start(bf16[128,2048]{1,0:T(8,128)(2,1)S(1)} %get-tuple-element.26), channel_id=1, source_target_pairs={{0,1},{1,0},{2,3},{3,2},{4,5},{5,4},{6,7},{7,6},{8,9},{9,8},{10,11... | collective-permute-start | bytes 1572872 | tf_op jit(solution)/shard_map/ppermute | solution.py:21
  69.2 5.5 %collective-permute-start.15 = (bf16[128,2048]{1,0:T(8,128)(2,1)S(1)}, bf16[128,2048]{1,0:T(8,128)(2,1)S(1)}, u32[]{:S(2)}, u32[]{:S(2)}) collective-permute-start(bf16[128,2048]{1,0:T(8,128)(2,1)S(1)} %get-tuple-element.28), channel_id=1, source_target_pairs={{0,1},{1,0},{2,3},{3,2},{4,5},{5,4},{6,7},{7,6},{8,9},{9,8},{10,11... | collective-permute-start | bytes 1572872 | tf_op jit(solution)/shard_map/ppermute | solution.py:21
  69.9 26.2 %collective-permute-start.5 = (bf16[64,2048]{1,0:T(8,128)(2,1)S(1)}, bf16[64,2048]{1,0:T(8,128)(2,1)S(1)}, u32[]{:S(2)}, u32[]{:S(2)}) collective-permute-start(bf16[64,2048]{1,0:T(8,128)(2,1)S(1)} %slice.71), channel_id=1, source_target_pairs={{0,2},{1,3},{2,0},{3,1},{4,6},{5,7},{6,4},{7,5},{8,10},{9,11},{10,... | collective-permute-start | bytes 786440 | tf_op jit(solution)/shard_map/ppermute | solution.py:21
  72.9 12.2 %collective-permute-start.21 = (bf16[128,2048]{1,0:T(8,128)(2,1)S(1)}, bf16[128,2048]{1,0:T(8,128)(2,1)S(1)}, u32[]{:S(2)}, u32[]{:S(2)}) collective-permute-start(bf16[128,2048]{1,0:T(8,128)(2,1)S(1)} %get-tuple-element.30), channel_id=1, source_target_pairs={{0,1},{1,0},{2,3},{3,2},{4,5},{5,4},{6,7},{7,6},{8,9},{9,8},{10,11... | collective-permute-start | bytes 1572872 | tf_op jit(solution)/shard_map/ppermute | solution.py:21
  73.4 10.1 %collective-permute-start.10 = (bf16[64,2048]{1,0:T(8,128)(2,1)S(1)}, bf16[64,2048]{1,0:T(8,128)(2,1)S(1)}, u32[]{:S(2)}, u32[]{:S(2)}) collective-permute-start(bf16[64,2048]{1,0:T(8,128)(2,1)S(1)} %slice.70), channel_id=1, source_target_pairs={{0,2},{1,3},{2,0},{3,1},{4,6},{5,7},{6,4},{7,5},{8,10},{9,11},{10,... | collective-permute-start | bytes 786440 | tf_op jit(solution)/shard_map/ppermute | solution.py:21
  74.8 14.2 %collective-permute-start.16 = (bf16[64,2048]{1,0:T(8,128)(2,1)S(1)}, bf16[64,2048]{1,0:T(8,128)(2,1)S(1)}, u32[]{:S(2)}, u32[]{:S(2)}) collective-permute-start(bf16[64,2048]{1,0:T(8,128)(2,1)S(1)} %slice.69), channel_id=1, source_target_pairs={{0,2},{1,3},{2,0},{3,1},{4,6},{5,7},{6,4},{7,5},{8,10},{9,11},{10,... | collective-permute-start | bytes 786440 | tf_op jit(solution)/shard_map/ppermute | solution.py:21
  83.5 12.6 %collective-permute-start.11 = (bf16[64,2048]{1,0:T(8,128)(2,1)S(1)}, bf16[64,2048]{1,0:T(8,128)(2,1)S(1)}, u32[]{:S(2)}, u32[]{:S(2)}) collective-permute-start(bf16[64,2048]{1,0:T(8,128)(2,1)S(1)} %fusion.2), channel_id=1, source_target_pairs={{0,4},{1,5},{2,6},{3,7},{4,0},{5,1},{6,2},{7,3},{8,12},{9,13},{10,... | collective-permute-start | bytes 786440 | tf_op jit(solution)/shard_map/ppermute | solution.py:21
  85.2 9.5 %collective-permute-start.22 = (bf16[64,2048]{1,0:T(8,128)(2,1)S(1)}, bf16[64,2048]{1,0:T(8,128)(2,1)S(1)}, u32[]{:S(2)}, u32[]{:S(2)}) collective-permute-start(bf16[64,2048]{1,0:T(8,128)(2,1)S(1)} %slice.68), channel_id=1, source_target_pairs={{0,2},{1,3},{2,0},{3,1},{4,6},{5,7},{6,4},{7,5},{8,10},{9,11},{10,... | collective-permute-start | bytes 786440 | tf_op jit(solution)/shard_map/ppermute | solution.py:21
  89.1 19.5 %collective-permute-start.17 = (bf16[64,2048]{1,0:T(8,128)(2,1)S(1)}, bf16[64,2048]{1,0:T(8,128)(2,1)S(1)}, u32[]{:S(2)}, u32[]{:S(2)}) collective-permute-start(bf16[64,2048]{1,0:T(8,128)(2,1)S(1)} %fusion.1), channel_id=1, source_target_pairs={{0,8},{1,9},{2,10},{3,11},{4,12},{5,13},{6,14},{7,15},{8,0},{9,1},... | collective-permute-start | bytes 786440 | tf_op jit(solution)/shard_map/ppermute | solution.py:21
  94.7 20.6 %collective-permute-start.23 = (bf16[64,2048]{1,0:T(8,128)(2,1)S(1)}, bf16[64,2048]{1,0:T(8,128)(2,1)S(1)}, u32[]{:S(2)}, u32[]{:S(2)}) collective-permute-start(bf16[64,2048]{1,0:T(8,128)(2,1)S(1)} %fusion), channel_id=1, source_target_pairs={{0,12},{1,13},{2,14},{3,15},{4,8},{5,9},{6,10},{7,11},{8,4},{9,5},... | collective-permute-start | bytes 786440 | tf_op jit(solution)/shard_map/ppermute | solution.py:21
where the time goes:
time: 116 us
  waiting for transfers between devices  55.9 us (48%)
  Pallas kernels  30.9 us (27%)
  starting transfers between devices  23.2 us (20%)
  other arithmetic  3.66 us (3%)
  local copies, waits for them, and re-layouts  2.34 us (2%)
    ppermute x24, waiting for transfers between devices, exchanged(): lax.ppermute(shard, axis, [(i, i ^ distance) for i in range(lax.axis_size...  55.9 us
    ppermute x24, starting transfers between devices, exchanged(): lax.ppermute(shard, axis, [(i, i ^ distance) for i in range(lax.axis_size...  23.2 us
    pallas_call x1, Pallas kernels, attend_cache(): pl.pallas_call(cache_kernel, grid=(KEY_VALUE_HEADS,), in_specs=[pl.BlockS...  19.7 us
    pallas_call x4, Pallas kernels, expert(): pl.pallas_call(functools.partial(expert_kernel, experts=experts), in_spec...  10.5 us
  transfers between devices with their start and end apart: 24, of which 12 were waited for; matrix products, arithmetic and copies ran while one was open for 3% of the time, Pallas kernels for 9%

commit v1 on v0

--- a/solution.py
+++ b/solution.py
@@ -27,7 +27,7 @@
 def cache_kernel(
     device_ref, lengths_ref, positions_ref, own_ref, visit_ref, row_k_ref, row_v_ref, cache_k_ref, cache_v_ref,
     own_out_ref, own_stats_ref, visit_out_ref,
-    closed, keys, values, stacked, result, shifts, stats,
+    keys, values, stacked, buffer, weights, result, shifts, stats,
 ):
     group = pl.program_id(0)
     rows = own_ref.shape[0]
@@ -51,65 +51,89 @@
             location = start + block * step + lax.broadcasted_iota(jnp.int32, (step, 1), 0)
             equal = jnp.where(location == marked, 1.0, 0.0).astype(jnp.bfloat16)
             count = jnp.dot(equal, counter, preferred_element_type=jnp.float32)
-            shut = ((count > 0.5) | (location >= length)) & (lane == HEAD_SIZE)
+            shut = ((count > 0.5) | (location >= length)) & (lane == 0)
             at = pl.ds(pl.multiple_of(block * step, step), step)
-            closed[at, :] = jnp.where(shut, score_masked_rows, 0.0).astype(jnp.bfloat16)
+            keys[at, LANES:] = jnp.where(shut, score_masked_rows, 0.0).astype(jnp.bfloat16)
             return carry
 
         lax.fori_loop(0, span // step, mark, 0)
         beyond = lax.broadcasted_iota(jnp.int32, (padded, 1), 0) >= rows
-        closed[span:, :] = jnp.where(beyond & (lane == HEAD_SIZE), score_masked_rows, 0.0).astype(jnp.bfloat16)
+        keys[span:, LANES:] = jnp.where(beyond & (lane == 0), score_masked_rows, 0.0).astype(jnp.bfloat16)
+        values[:, LANES:] = jnp.ones((key_count, LANES), jnp.bfloat16)
+        stacked[:, LANES:] = jnp.where(
+            lax.broadcasted_iota(jnp.int32, (stacked.shape[0], LANES), 1) == 0, 1.0, 0.0
+        ).astype(jnp.bfloat16)
         stats[...] = jnp.zeros_like(stats)
         if padded > rows:
-            keys[span + rows :, :] = closed[span + rows :, :]
-            values[span + rows :, :] = jnp.zeros((padded - rows, LANES), jnp.bfloat16)
+            keys[span + rows :, :LANES] = jnp.zeros((padded - rows, LANES), jnp.bfloat16)
+            values[span + rows :, :LANES] = jnp.zeros((padded - rows, LANES), jnp.bfloat16)
+
+    @pl.when(group % 2 == 0)
+    def _():
+        keys[:span, :LANES] = cache_k_ref[...]
+        values[:span, :LANES] = cache_v_ref[...]
+        keys[span : span + rows, :LANES] = row_k_ref[...]
+        values[span : span + rows, :LANES] = row_v_ref[...]
 
     first = group % 2 == 0
-    zero = jnp.bfloat16(0.0)
-    one = jnp.bfloat16(1.0)
-
-    def placed(block, rest):
-        wide = block.astype(jnp.float32)
-        moved = jnp.where(first, wide, pltpu.roll(wide, HEAD_SIZE, 1)).astype(jnp.bfloat16)
-        return jnp.where(low, moved, rest)
-
-    keys[:span, :] = placed(cache_k_ref[...], closed[:span, :])
-    values[:span, :] = placed(cache_v_ref[...], one)
-    keys[span : span + rows, :] = placed(row_k_ref[...], zero)
-    values[span : span + rows, :] = placed(row_v_ref[...], one)
+    side = low == first
     scale = 1.0 / math.sqrt(HEAD_SIZE)
-    marker = jnp.where(lane == HEAD_SIZE, 1.0, 0.0)
     for pair in range(pairs):
         for source, ref in enumerate((own_ref, visit_ref)):
             query = ref[:, pair * LANES : (pair + 1) * LANES].astype(jnp.float32) * scale
+            turned = pltpu.roll(query, HEAD_SIZE, 1)
             for parity in range(2):
                 base = ((parity * pairs + pair) * 2 + source) * rows
-                moved = query if parity == 0 else pltpu.roll(query, HEAD_SIZE, 1)
-                stacked[base : base + rows, :] = jnp.where(low, moved, marker).astype(jnp.bfloat16)
-
-    chunk = 4 * rows
-    for begin in range(0, stacked.shape[0], chunk):
-        at = slice(begin, begin + chunk)
-        scores = lax.dot_general(
-            stacked[at, :], keys[...], (((1,), (1,)), ((), ())), preferred_element_type=jnp.float32
-        )
-        shift = jnp.max(scores, axis=1, keepdims=True).astype(jnp.bfloat16).astype(jnp.float32)
-        weights = jnp.exp(scores - shift).astype(jnp.bfloat16)
-        result[at, :] = jnp.dot(weights, values[...], preferred_element_type=jnp.float32)
+                moved = jnp.where(first == (parity == 0), query, turned)
+                stacked[base : base + rows, :LANES] = jnp.where(side, moved, 0.0).astype(jnp.bfloat16)
+
+    chunk = buffer.shape[1]
+    wide = 2 * LANES
+
+    def score(turn):
+        query = stacked[turn * chunk : (turn + 1) * chunk, :]
+        highest = None
+        for begin in range(0, key_count, wide):
+            end = min(begin + wide, key_count)
+            tile = lax.dot_general(
+                query, keys[begin:end, :], (((1,), (1,)), ((), ())), preferred_element_type=jnp.float32
+            )
+            buffer[turn % 2, :, begin:end] = tile
+            for lanes in range(0, end - begin, LANES):
+                part = tile[:, lanes : lanes + LANES]
+                highest = part if highest is None else jnp.maximum(highest, part)
+        return jnp.max(highest, axis=1, keepdims=True).astype(jnp.bfloat16).astype(jnp.float32)
+
+    def weigh(turn, shift):
+        at = slice(turn * chunk, (turn + 1) * chunk)
         shifts[at, :] = jnp.broadcast_to(shift, (chunk, LANES))
+        for begin in range(0, key_count, wide):
+            end = min(begin + wide, key_count)
+            weights[turn % 2, :, begin:end] = jnp.exp(buffer[turn % 2, :, begin:end] - shift).astype(jnp.bfloat16)
+        result[at, :] = jnp.dot(weights[turn % 2], values[...], preferred_element_type=jnp.float32)
+
+    turns = stacked.shape[0] // chunk
+    shift = score(0)
+    for turn in range(turns):
+        ahead = score(turn + 1) if turn + 1 < turns else None
+        weigh(turn, shift)
+        shift = ahead
 
     both = 2 * rows
     seen = stats[...]
     for pair in range(pairs):
         even = slice(pair * both, (pair + 1) * both)
         odd = slice((pairs + pair) * both, (pairs + pair + 1) * both)
-        joined = jnp.where(low, result[even, :], pltpu.roll(result[odd, :], HEAD_SIZE, 1))
+        left, right = result[even, :LANES], result[odd, :LANES]
+        left = jnp.where(first, left, pltpu.roll(left, HEAD_SIZE, 1))
+        right = jnp.where(first, pltpu.roll(right, HEAD_SIZE, 1), right)
+        joined = jnp.where(low, left, right)
         own_out_ref[:, pair * LANES : (pair + 1) * LANES] = joined[:rows]
         column = pl.multiple_of((group * pairs + pair) * LANES, LANES)
         visit_out_ref[:, pl.ds(column, LANES)] = joined[rows:].astype(jnp.bfloat16)
         for parity, at in enumerate((even, odd)):
             head = (group * pairs + pair) * 2 + parity
-            total = result[at, :]
+            total = result[at, LANES:]
             high = total.astype(jnp.bfloat16).astype(jnp.float32)
             seen = jnp.where(lane == head, shifts[at, :], seen)
             seen = jnp.where(lane == head + 2 * QUERY_HEADS, high, seen)
@@ -131,7 +155,8 @@
     half = KEY_VALUE_HEADS * HEAD_SIZE // LANES
     per_block = LANES // HEAD_SIZE
     in_hbm = functools.partial(pltpu.with_memory_space_constraint, memory_space=pltpu.HBM)
-    own, row_key_value, key_value_cache, positions = map(in_hbm, (own, row_key_value, key_value_cache, positions))
+    own, row_key_value, key_value_cache = map(in_hbm, (own, row_key_value, key_value_cache))
+    lengths, positions = in_hbm(lengths), in_hbm(positions)
     return pl.pallas_call(
         cache_kernel,
         grid=(KEY_VALUE_HEADS,),
@@ -157,11 +182,12 @@
             jax.ShapeDtypeStruct((rows, width + LANES), jnp.bfloat16),
         ],
         scratch_shapes=[
-            pltpu.VMEM((key_count, LANES), jnp.bfloat16),
-            pltpu.VMEM((key_count, LANES), jnp.bfloat16),
-            pltpu.VMEM((key_count, LANES), jnp.bfloat16),
-            pltpu.VMEM((stack, LANES), jnp.bfloat16),
-            pltpu.VMEM((stack, LANES), jnp.float32),
+            pltpu.VMEM((key_count, 2 * LANES), jnp.bfloat16),
+            pltpu.VMEM((key_count, 2 * LANES), jnp.bfloat16),
+            pltpu.VMEM((stack, 2 * LANES), jnp.bfloat16),
+            pltpu.VMEM((2, 4 * rows, key_count), jnp.float32),
+            pltpu.VMEM((2, 4 * rows, key_count), jnp.bfloat16),
+            pltpu.VMEM((stack, 2 * LANES), jnp.float32),
             pltpu.VMEM((stack, LANES), jnp.float32),
             pltpu.VMEM((2 * rows, LANES), jnp.float32),
         ],

time: 116 us -> 113 us (0.974)
  Pallas kernels: 30.9 us -> 28.5 us
    pallas_call x1, Pallas kernels: 19.7 us -> 17.3 us  [attend_cache(): pl.pallas_call(cache_kernel, grid=(KEY_VALUE_HEADS,), in_specs=[pl.BlockS...]
where the time goes in v1:
time: 113 us
  waiting for transfers between devices  55.8 us (49%)
  Pallas kernels  28.5 us (25%)
  starting transfers between devices  23.2 us (21%)
  other arithmetic  3.66 us (3%)
  local copies, waits for them, and re-layouts  1.54 us (1%)
    ppermute x24, waiting for transfers between devices, exchanged(): lax.ppermute(shard, axis, [(i, i ^ distance) for i in range(lax.axis_size...  55.8 us
    ppermute x24, starting transfers between devices, exchanged(): lax.ppermute(shard, axis, [(i, i ^ distance) for i in range(lax.axis_size...  23.2 us
    pallas_call x1, Pallas kernels, attend_cache(): pl.pallas_call(cache_kernel, grid=(KEY_VALUE_HEADS,), in_specs=[pl.BlockS...  17.3 us
    pallas_call x4, Pallas kernels, expert(): pl.pallas_call(functools.partial(expert_kernel, experts=experts), in_spec...  10.5 us
  transfers between devices with their start and end apart: 24, of which 12 were waited for; matrix products, arithmetic and copies ran while one was open for 3% of the time, Pallas kernels for 9%

profile of v1, /device:TPU:15, one launch (start us, length us, event | category | flops | bytes accessed | tf_op | source)
XLA Modules:
  0.0 113.0 jit_solution(14888696287278549675)
XLA Ops:
  0.0 0.7 collective-permute-start
  0.7 0.7 reduce_sum.18
  1.4 0.7 broadcast_divide_fusion
  2.1 0.7 select_reduce_fusion
  3.0 17.3 %cache_attention.1 = (f32[64,2048]{1,0:T(8,128)S(1)}, bf16[64,128]{1,0:T(8,128)(2,1)S(1)}, bf16[64,2176]{1,0:T(8,128)(2,1)S(1)}) custom-call(s32[1]{0:T(128)} %bitcast.device_ref, s32[8]{0:T(128)} %lengths_ref.1, s32[8,128]{1,0:T(8,128)} %positions_ref.1, bf16[64,2048]{1,0:T(8,128)(2,1)} %own_ref.1, bf16[64,2048]{1,0:T(8,128)(2,1)S(1)} %collective-permute-done.visit_ref, ...), custom_call_target="tpu_custom_call" | custom-call | tf_op jit(solution)/shard_map/cache_attention/pallas_call | solution.py:160
  20.6 1.4 %collective-permute-done.1.far_ref = bf16[64,2176]{1,0:T(8,128)(2,1)S(1)} collective-permute-done((bf16[64,2176]{1,0:T(8,128)(2,1)S(1)}, bf16[64,2176]{1,0:T(8,128)(2,1)S(1)}, u32[]{:S(2)}, u32[]{:S(2)}) %collective-permute-start.1) | collective-permute-done | bytes 278560 | tf_op jit(solution)/shard_map/ppermute | solution.py:21
  21.9 0.9 copy-done.3
  22.9 0.8 merge_norm.1
  23.7 0.2 collective-permute-start.6
  23.9 2.3 %collective-permute-start.12 = (bf16[64,2176]{1,0:T(8,128)(2,1)S(1)}, bf16[64,2176]{1,0:T(8,128)(2,1)S(1)}, u32[]{:S(2)}, u32[]{:S(2)}) collective-permute-start(bf16[64,2176]{1,0:T(8,128)(2,1)S(1)} %get-tuple-element.22), channel_id=1, source_target_pairs={{0,8},{1,9},{2,10},{3,11},{4,12},{5,13},{6,14},{7,15},{8,0},{9,1},... | collective-permute-start | bytes 835592 | tf_op jit(solution)/shard_map/ppermute | solution.py:21
  26.2 0.2 collective-permute-start.2
  26.5 7.3 %collective-permute-done.2 = bf16[64,2176]{1,0:T(8,128)(2,1)S(1)} collective-permute-done((bf16[64,2176]{1,0:T(8,128)(2,1)S(1)}, bf16[64,2176]{1,0:T(8,128)(2,1)S(1)}, u32[]{:S(2)}, u32[]{:S(2)}) %collective-permute-start.2) | collective-permute-done | bytes 278560 | tf_op jit(solution)/shard_map/ppermute | solution.py:21
  33.8 1.6 %collective-permute-start.3 = (bf16[128,2176]{1,0:T(8,128)(2,1)S(1)}, bf16[128,2176]{1,0:T(8,128)(2,1)S(1)}, u32[]{:S(2)}, u32[]{:S(2)}) collective-permute-start(bf16[128,2176]{1,0:T(8,128)(2,1)S(1)} %constant_dynamic-update-slice_fusion.near_ref), channel_id=1, source_target_pairs={{0,1},{1,0},{2,3},{3,2},{4,5},{5,4},{6,7},{7,6},{8,9},{9,8},{10,11... | collective-permute-start | bytes 1671176 | tf_op jit(solution)/shard_map/ppermute | solution.py:21
  35.4 0.3 collective-permute-done.6
  35.6 0.2 collective-permute-start.7
  35.9 3.0 %collective-permute-done.12 = bf16[64,2176]{1,0:T(8,128)(2,1)S(1)} collective-permute-done((bf16[64,2176]{1,0:T(8,128)(2,1)S(1)}, bf16[64,2176]{1,0:T(8,128)(2,1)S(1)}, u32[]{:S(2)}, u32[]{:S(2)}) %collective-permute-start.12) | collective-permute-done | bytes 278560 | tf_op jit(solution)/shard_map/ppermute | solution.py:21
  38.9 0.2 collective-permute-start.13
  39.1 0.3 collective-permute-start.18
  39.4 3.4 %collective-permute-done.7 = bf16[64,2176]{1,0:T(8,128)(2,1)S(1)} collective-permute-done((bf16[64,2176]{1,0:T(8,128)(2,1)S(1)}, bf16[64,2176]{1,0:T(8,128)(2,1)S(1)}, u32[]{:S(2)}, u32[]{:S(2)}) %collective-permute-start.7) | collective-permute-done | bytes 278560 | tf_op jit(solution)/shard_map/ppermute | solution.py:21
  42.9 3.4 %collective-permute-start.8 = (bf16[128,2176]{1,0:T(8,128)(2,1)S(1)}, bf16[128,2176]{1,0:T(8,128)(2,1)S(1)}, u32[]{:S(2)}, u32[]{:S(2)}) collective-permute-start(bf16[128,2176]{1,0:T(8,128)(2,1)S(1)} %constant_dynamic-update-slice_fusion.2.near_ref), channel_id=1, source_target_pairs={{0,1},{1,0},{2,3},{3,2},{4,5},{5,4},{6,7},{7,6},{8,9},{9,8},{10,11... | collective-permute-start | bytes 1671176 | tf_op jit(solution)/shard_map/ppermute | solution.py:21
  46.3 2.6 %collective-permute-done.13 = bf16[64,2176]{1,0:T(8,128)(2,1)S(1)} collective-permute-done((bf16[64,2176]{1,0:T(8,128)(2,1)S(1)}, bf16[64,2176]{1,0:T(8,128)(2,1)S(1)}, u32[]{:S(2)}, u32[]{:S(2)}) %collective-permute-start.13) | collective-permute-done | bytes 278560 | tf_op jit(solution)/shard_map/ppermute | solution.py:21
  48.9 1.9 %collective-permute-start.14 = (bf16[128,2176]{1,0:T(8,128)(2,1)S(1)}, bf16[128,2176]{1,0:T(8,128)(2,1)S(1)}, u32[]{:S(2)}, u32[]{:S(2)}) collective-permute-start(bf16[128,2176]{1,0:T(8,128)(2,1)S(1)} %constant_dynamic-update-slice_fusion.4.near_ref), channel_id=1, source_target_pairs={{0,1},{1,0},{2,3},{3,2},{4,5},{5,4},{6,7},{7,6},{8,9},{9,8},{10,11... | collective-permute-start | bytes 1671176 | tf_op jit(solution)/shard_map/ppermute | solution.py:21
  50.8 2.2 %collective-permute-start.19 = (bf16[64,2176]{1,0:T(8,128)(2,1)S(1)}, bf16[64,2176]{1,0:T(8,128)(2,1)S(1)}, u32[]{:S(2)}, u32[]{:S(2)}) collective-permute-start(bf16[64,2176]{1,0:T(8,128)(2,1)S(1)} %collective-permute-done.13), channel_id=1, source_target_pairs={{0,4},{1,5},{2,6},{3,7},{4,0},{5,1},{6,2},{7,3},{8,12},{9,13},{10,... | collective-permute-start | bytes 835592 | tf_op jit(solution)/shard_map/ppermute | solution.py:21
  53.0 2.6 %expert.4 = (f32[128,2048]{1,0:T(8,128)S(1)}, bf16[128,2048]{1,0:T(8,128)(2,1)S(1)}) custom-call(s32[1]{0:T(128)} %bitcast.device_ref, bf16[128,2176]{1,0:T(8,128)(2,1)S(1)} %constant_dynamic-update-slice_fusion.near_ref, bf16[128,2176]{1,0:T(8,128)(2,1)S(1)} %collective-permute-done.3.far_ref, bf16[1,2048,768]{2,1,0:T(8,128)(2,1)S(1)} %copy-done, ...), custom_call_target="tpu_custom_call" | custom-call | tf_op jit(solution)/shard_map/expert/pallas_call | solution.py:279
  55.6 0.4 collective-permute-start.4
  56.1 3.9 %collective-permute-done.19 = bf16[64,2176]{1,0:T(8,128)(2,1)S(1)} collective-permute-done((bf16[64,2176]{1,0:T(8,128)(2,1)S(1)}, bf16[64,2176]{1,0:T(8,128)(2,1)S(1)}, u32[]{:S(2)}, u32[]{:S(2)}) %collective-permute-start.19) | collective-permute-done | bytes 278560 | tf_op jit(solution)/shard_map/ppermute | solution.py:21
  60.0 0.7 collective-permute-start.20
  60.7 2.6 %expert.5 = (f32[128,2048]{1,0:T(8,128)S(1)}, bf16[128,2048]{1,0:T(8,128)(2,1)S(1)}) custom-call(s32[1]{0:T(128)} %bitcast.device_ref, bf16[128,2176]{1,0:T(8,128)(2,1)S(1)} %constant_dynamic-update-slice_fusion.2.near_ref, bf16[128,2176]{1,0:T(8,128)(2,1)S(1)} %collective-permute-done.8.far_ref, bf16[1,2048,768]{2,1,0:T(8,128)(2,1)S(1)} %copy-done, ...), custom_call_target="tpu_custom_call" | custom-call | tf_op jit(solution)/shard_map/expert/pallas_call | solution.py:279
  63.4 2.6 %expert.6 = (f32[128,2048]{1,0:T(8,128)S(1)}, bf16[128,2048]{1,0:T(8,128)(2,1)S(1)}) custom-call(s32[1]{0:T(128)} %bitcast.device_ref, bf16[128,2176]{1,0:T(8,128)(2,1)S(1)} %constant_dynamic-update-slice_fusion.4.near_ref, bf16[128,2176]{1,0:T(8,128)(2,1)S(1)} %collective-permute-done.14.far_ref, bf16[1,2048,768]{2,1,0:T(8,128)(2,1)S(1)} %copy-done, ...), custom_call_target="tpu_custom_call" | custom-call | tf_op jit(solution)/shard_map/expert/pallas_call | solution.py:279
  66.0 0.6 collective-permute-start.15
  66.6 0.1 convert_add_fusion.3
  66.7 0.3 collective-permute-start.5
  67.0 2.6 %expert.7 = (f32[128,2048]{1,0:T(8,128)S(1)}, bf16[128,2048]{1,0:T(8,128)(2,1)S(1)}) custom-call(s32[1]{0:T(128)} %bitcast.device_ref, bf16[128,2176]{1,0:T(8,128)(2,1)S(1)} %constant_dynamic-update-slice_fusion.6.near_ref, bf16[128,2176]{1,0:T(8,128)(2,1)S(1)} %collective-permute-done.20.far_ref, bf16[1,2048,768]{2,1,0:T(8,128)(2,1)S(1)} %copy-done, ...), custom_call_target="tpu_custom_call" | custom-call | tf_op jit(solution)/shard_map/expert/pallas_call | solution.py:279
  69.6 0.4 collective-permute-start.21
  70.0 0.1 convert_add_fusion.2
  70.2 1.3 %collective-permute-start.10 = (bf16[64,2048]{1,0:T(8,128)(2,1)S(1)}, bf16[64,2048]{1,0:T(8,128)(2,1)S(1)}, u32[]{:S(2)}, u32[]{:S(2)}) collective-permute-start(bf16[64,2048]{1,0:T(8,128)(2,1)S(1)} %slice.70), channel_id=1, source_target_pairs={{0,2},{1,3},{2,0},{3,1},{4,6},{5,7},{6,4},{7,5},{8,10},{9,11},{10,... | collective-permute-start | bytes 786440 | tf_op jit(solution)/shard_map/ppermute | solution.py:21
  71.5 0.1 convert_add_fusion.1
  71.6 0.3 collective-permute-start.16
  71.9 8.3 %collective-permute-done.10 = bf16[64,2048]{1,0:T(8,128)(2,1)S(1)} collective-permute-done((bf16[64,2048]{1,0:T(8,128)(2,1)S(1)}, bf16[64,2048]{1,0:T(8,128)(2,1)S(1)}, u32[]{:S(2)}, u32[]{:S(2)}) %collective-permute-start.10) | collective-permute-done | bytes 262176 | tf_op jit(solution)/shard_map/ppermute | solution.py:21
  80.3 1.5 %collective-permute-start.11 = (bf16[64,2048]{1,0:T(8,128)(2,1)S(1)}, bf16[64,2048]{1,0:T(8,128)(2,1)S(1)}, u32[]{:S(2)}, u32[]{:S(2)}) collective-permute-start(bf16[64,2048]{1,0:T(8,128)(2,1)S(1)} %fusion.2), channel_id=1, source_target_pairs={{0,4},{1,5},{2,6},{3,7},{4,0},{5,1},{6,2},{7,3},{8,12},{9,13},{10,... | collective-permute-start | bytes 786440 | tf_op jit(solution)/shard_map/ppermute | solution.py:21
  82.0 0.3 collective-permute-start.22
  82.3 3.6 %collective-permute-done.16 = bf16[64,2048]{1,0:T(8,128)(2,1)S(1)} collective-permute-done((bf16[64,2048]{1,0:T(8,128)(2,1)S(1)}, bf16[64,2048]{1,0:T(8,128)(2,1)S(1)}, u32[]{:S(2)}, u32[]{:S(2)}) %collective-permute-start.16) | collective-permute-done | bytes 262176 | tf_op jit(solution)/shard_map/ppermute | solution.py:21
  85.9 2.6 %collective-permute-start.17 = (bf16[64,2048]{1,0:T(8,128)(2,1)S(1)}, bf16[64,2048]{1,0:T(8,128)(2,1)S(1)}, u32[]{:S(2)}, u32[]{:S(2)}) collective-permute-start(bf16[64,2048]{1,0:T(8,128)(2,1)S(1)} %fusion.1), channel_id=1, source_target_pairs={{0,8},{1,9},{2,10},{3,11},{4,12},{5,13},{6,14},{7,15},{8,0},{9,1},... | collective-permute-start | bytes 786440 | tf_op jit(solution)/shard_map/ppermute | solution.py:21
  88.5 3.0 %collective-permute-done.22 = bf16[64,2048]{1,0:T(8,128)(2,1)S(1)} collective-permute-done((bf16[64,2048]{1,0:T(8,128)(2,1)S(1)}, bf16[64,2048]{1,0:T(8,128)(2,1)S(1)}, u32[]{:S(2)}, u32[]{:S(2)}) %collective-permute-start.22) | collective-permute-done | bytes 262176 | tf_op jit(solution)/shard_map/ppermute | solution.py:21
  91.5 1.4 %collective-permute-start.23 = (bf16[64,2048]{1,0:T(8,128)(2,1)S(1)}, bf16[64,2048]{1,0:T(8,128)(2,1)S(1)}, u32[]{:S(2)}, u32[]{:S(2)}) collective-permute-start(bf16[64,2048]{1,0:T(8,128)(2,1)S(1)} %fusion), channel_id=1, source_target_pairs={{0,12},{1,13},{2,14},{3,15},{4,8},{5,9},{6,10},{7,11},{8,4},{9,5},... | collective-permute-start | bytes 786440 | tf_op jit(solution)/shard_map/ppermute | solution.py:21
  92.9 12.6 %collective-permute-done.17 = bf16[64,2048]{1,0:T(8,128)(2,1)S(1)} collective-permute-done((bf16[64,2048]{1,0:T(8,128)(2,1)S(1)}, bf16[64,2048]{1,0:T(8,128)(2,1)S(1)}, u32[]{:S(2)}, u32[]{:S(2)}) %collective-permute-start.17) | collective-permute-done | bytes 262176 | tf_op jit(solution)/shard_map/ppermute | solution.py:21
  105.5 6.6 %collective-permute-done.23 = bf16[64,2048]{1,0:T(8,128)(2,1)S(1)} collective-permute-done((bf16[64,2048]{1,0:T(8,128)(2,1)S(1)}, bf16[64,2048]{1,0:T(8,128)(2,1)S(1)}, u32[]{:S(2)}, u32[]{:S(2)}) %collective-permute-start.23) | collective-permute-done | bytes 262176 | tf_op jit(solution)/shard_map/ppermute | solution.py:21
  112.1 0.9 fusion.7
  (46 shorter events, 1.1 us)
Async XLA Ops:
  0.0 21.9 %copy-start.4 = (f32[2048]{0:T(1024)S(1)}, f32[2048]{0:T(1024)}, u32[]{:S(2)}) copy-start(f32[2048]{0:T(1024)} %param.16) | copy-start | bytes 24580
  0.0 3.0 %collective-permute-start = (bf16[64,2048]{1,0:T(8,128)(2,1)}, bf16[64,2048]{1,0:T(8,128)(2,1)S(1)}, u32[]{:S(2)}, u32[]{:S(2)}) collective-permute-start(bf16[64,2048]{1,0:T(8,128)(2,1)} %own_ref.1), channel_id=1, source_target_pairs={{0,1},{1,0},{2,3},{3,2},{4,5},{5,4},{6,7},{7,6},{8,9},{9,8},{10,11... | collective-permute-start | bytes 786440 | tf_op jit(solution)/shard_map/ppermute | solution.py:21
  2.9 50.1 %copy-start.2 = (bf16[1,768,2048]{2,1,0:T(8,128)(2,1)S(1)}, bf16[1,768,2048]{2,1,0:T(8,128)(2,1)}, u32[]{:S(2)}) copy-start(bf16[1,768,2048]{2,1,0:T(8,128)(2,1)} %down_ref.7) | copy-start | bytes 9437188
  3.0 50.0 %copy-start.1 = (bf16[1,2048,768]{2,1,0:T(8,128)(2,1)S(1)}, bf16[1,2048,768]{2,1,0:T(8,128)(2,1)}, u32[]{:S(2)}) copy-start(bf16[1,2048,768]{2,1,0:T(8,128)(2,1)} %up_ref.7) | copy-start | bytes 9437188
  20.3 32.7 %copy-start = (bf16[1,2048,768]{2,1,0:T(8,128)(2,1)S(1)}, bf16[1,2048,768]{2,1,0:T(8,128)(2,1)}, u32[]{:S(2)}) copy-start(bf16[1,2048,768]{2,1,0:T(8,128)(2,1)} %gate_ref.7) | copy-start | bytes 9437188
  20.3 1.6 %collective-permute-start.1 = (bf16[64,2176]{1,0:T(8,128)(2,1)S(1)}, bf16[64,2176]{1,0:T(8,128)(2,1)S(1)}, u32[]{:S(2)}, u32[]{:S(2)}) collective-permute-start(bf16[64,2176]{1,0:T(8,128)(2,1)S(1)} %get-tuple-element.20), channel_id=1, source_target_pairs={{0,1},{1,0},{2,3},{3,2},{4,5},{5,4},{6,7},{7,6},{8,9},{9,8},{10,11... | collective-permute-start | bytes 835592 | tf_op jit(solution)/shard_map/ppermute | solution.py:21
  21.9 1.0 copy-start.3
  23.7 12.0 %collective-permute-start.6 = (bf16[64,2176]{1,0:T(8,128)(2,1)S(1)}, bf16[64,2176]{1,0:T(8,128)(2,1)S(1)}, u32[]{:S(2)}, u32[]{:S(2)}) collective-permute-start(bf16[64,2176]{1,0:T(8,128)(2,1)S(1)} %get-tuple-element.22), channel_id=1, source_target_pairs={{0,4},{1,5},{2,6},{3,7},{4,0},{5,1},{6,2},{7,3},{8,12},{9,13},{10,... | collective-permute-start | bytes 835592 | tf_op jit(solution)/shard_map/ppermute | solution.py:21
  23.9 14.9 %collective-permute-start.12 = (bf16[64,2176]{1,0:T(8,128)(2,1)S(1)}, bf16[64,2176]{1,0:T(8,128)(2,1)S(1)}, u32[]{:S(2)}, u32[]{:S(2)}) collective-permute-start(bf16[64,2176]{1,0:T(8,128)(2,1)S(1)} %get-tuple-element.22), channel_id=1, source_target_pairs={{0,8},{1,9},{2,10},{3,11},{4,12},{5,13},{6,14},{7,15},{8,0},{9,1},... | collective-permute-start | bytes 835592 | tf_op jit(solution)/shard_map/ppermute | solution.py:21
  26.2 7.5 %collective-permute-start.2 = (bf16[64,2176]{1,0:T(8,128)(2,1)S(1)}, bf16[64,2176]{1,0:T(8,128)(2,1)S(1)}, u32[]{:S(2)}, u32[]{:S(2)}) collective-permute-start(bf16[64,2176]{1,0:T(8,128)(2,1)S(1)} %get-tuple-element.22), channel_id=1, source_target_pairs={{0,2},{1,3},{2,0},{3,1},{4,6},{5,7},{6,4},{7,5},{8,10},{9,11},{10,... | collective-permute-start | bytes 835592 | tf_op jit(solution)/shard_map/ppermute | solution.py:21
  33.8 19.2 %collective-permute-start.3 = (bf16[128,2176]{1,0:T(8,128)(2,1)S(1)}, bf16[128,2176]{1,0:T(8,128)(2,1)S(1)}, u32[]{:S(2)}, u32[]{:S(2)}) collective-permute-start(bf16[128,2176]{1,0:T(8,128)(2,1)S(1)} %constant_dynamic-update-slice_fusion.near_ref), channel_id=1, source_target_pairs={{0,1},{1,0},{2,3},{3,2},{4,5},{5,4},{6,7},{7,6},{8,9},{9,8},{10,11... | collective-permute-start | bytes 1671176 | tf_op jit(solution)/shard_map/ppermute | solution.py:21
  35.6 7.2 %collective-permute-start.7 = (bf16[64,2176]{1,0:T(8,128)(2,1)S(1)}, bf16[64,2176]{1,0:T(8,128)(2,1)S(1)}, u32[]{:S(2)}, u32[]{:S(2)}) collective-permute-start(bf16[64,2176]{1,0:T(8,128)(2,1)S(1)} %collective-permute-done.6), channel_id=1, source_target_pairs={{0,2},{1,3},{2,0},{3,1},{4,6},{5,7},{6,4},{7,5},{8,10},{9,11},{10,... | collective-permute-start | bytes 835592 | tf_op jit(solution)/shard_map/ppermute | solution.py:21
  38.9 10.0 %collective-permute-start.13 = (bf16[64,2176]{1,0:T(8,128)(2,1)S(1)}, bf16[64,2176]{1,0:T(8,128)(2,1)S(1)}, u32[]{:S(2)}, u32[]{:S(2)}) collective-permute-start(bf16[64,2176]{1,0:T(8,128)(2,1)S(1)} %collective-permute-done.12), channel_id=1, source_target_pairs={{0,2},{1,3},{2,0},{3,1},{4,6},{5,7},{6,4},{7,5},{8,10},{9,11},{10,... | collective-permute-start | bytes 835592 | tf_op jit(solution)/shard_map/ppermute | solution.py:21
  39.1 17.0 %collective-permute-start.18 = (bf16[64,2176]{1,0:T(8,128)(2,1)S(1)}, bf16[64,2176]{1,0:T(8,128)(2,1)S(1)}, u32[]{:S(2)}, u32[]{:S(2)}) collective-permute-start(bf16[64,2176]{1,0:T(8,128)(2,1)S(1)} %collective-permute-done.12), channel_id=1, source_target_pairs={{0,4},{1,5},{2,6},{3,7},{4,0},{5,1},{6,2},{7,3},{8,12},{9,13},{10,... | collective-permute-start | bytes 835592 | tf_op jit(solution)/shard_map/ppermute | solution.py:21
  42.9 17.8 %collective-permute-start.8 = (bf16[128,2176]{1,0:T(8,128)(2,1)S(1)}, bf16[128,2176]{1,0:T(8,128)(2,1)S(1)}, u32[]{:S(2)}, u32[]{:S(2)}) collective-permute-start(bf16[128,2176]{1,0:T(8,128)(2,1)S(1)} %constant_dynamic-update-slice_fusion.2.near_ref), channel_id=1, source_target_pairs={{0,1},{1,0},{2,3},{3,2},{4,5},{5,4},{6,7},{7,6},{8,9},{9,8},{10,11... | collective-permute-start | bytes 1671176 | tf_op jit(solution)/shard_map/ppermute | solution.py:21
  48.9 14.5 %collective-permute-start.14 = (bf16[128,2176]{1,0:T(8,128)(2,1)S(1)}, bf16[128,2176]{1,0:T(8,128)(2,1)S(1)}, u32[]{:S(2)}, u32[]{:S(2)}) collective-permute-start(bf16[128,2176]{1,0:T(8,128)(2,1)S(1)} %constant_dynamic-update-slice_fusion.4.near_ref), channel_id=1, source_target_pairs={{0,1},{1,0},{2,3},{3,2},{4,5},{5,4},{6,7},{7,6},{8,9},{9,8},{10,11... | collective-permute-start | bytes 1671176 | tf_op jit(solution)/shard_map/ppermute | solution.py:21
  50.8 9.2 %collective-permute-start.19 = (bf16[64,2176]{1,0:T(8,128)(2,1)S(1)}, bf16[64,2176]{1,0:T(8,128)(2,1)S(1)}, u32[]{:S(2)}, u32[]{:S(2)}) collective-permute-start(bf16[64,2176]{1,0:T(8,128)(2,1)S(1)} %collective-permute-done.13), channel_id=1, source_target_pairs={{0,4},{1,5},{2,6},{3,7},{4,0},{5,1},{6,2},{7,3},{8,12},{9,13},{10,... | collective-permute-start | bytes 835592 | tf_op jit(solution)/shard_map/ppermute | solution.py:21
  55.6 10.9 %collective-permute-start.4 = (bf16[128,2048]{1,0:T(8,128)(2,1)S(1)}, bf16[128,2048]{1,0:T(8,128)(2,1)S(1)}, u32[]{:S(2)}, u32[]{:S(2)}) collective-permute-start(bf16[128,2048]{1,0:T(8,128)(2,1)S(1)} %get-tuple-element.24), channel_id=1, source_target_pairs={{0,1},{1,0},{2,3},{3,2},{4,5},{5,4},{6,7},{7,6},{8,9},{9,8},{10,11... | collective-permute-start | bytes 1572872 | tf_op jit(solution)/shard_map/ppermute | solution.py:21
  60.0 7.1 %collective-permute-start.20 = (bf16[128,2176]{1,0:T(8,128)(2,1)S(1)}, bf16[128,2176]{1,0:T(8,128)(2,1)S(1)}, u32[]{:S(2)}, u32[]{:S(2)}) collective-permute-start(bf16[128,2176]{1,0:T(8,128)(2,1)S(1)} %constant_dynamic-update-slice_fusion.6.near_ref), channel_id=1, source_target_pairs={{0,1},{1,0},{2,3},{3,2},{4,5},{5,4},{6,7},{7,6},{8,9},{9,8},{10,11... | collective-permute-start | bytes 1671176 | tf_op jit(solution)/shard_map/ppermute | solution.py:21
  63.3 6.7 %collective-permute-start.9 = (bf16[128,2048]{1,0:T(8,128)(2,1)S(1)}, bf16[128,2048]{1,0:T(8,128)(2,1)S(1)}, u32[]{:S(2)}, u32[]{:S(2)}) collective-permute-start(bf16[128,2048]{1,0:T(8,128)(2,1)S(1)} %get-tuple-element.26), channel_id=1, source_target_pairs={{0,1},{1,0},{2,3},{3,2},{4,5},{5,4},{6,7},{7,6},{8,9},{9,8},{10,11... | collective-permute-start | bytes 1572872 | tf_op jit(solution)/shard_map/ppermute | solution.py:21
  66.0 5.5 %collective-permute-start.15 = (bf16[128,2048]{1,0:T(8,128)(2,1)S(1)}, bf16[128,2048]{1,0:T(8,128)(2,1)S(1)}, u32[]{:S(2)}, u32[]{:S(2)}) collective-permute-start(bf16[128,2048]{1,0:T(8,128)(2,1)S(1)} %get-tuple-element.28), channel_id=1, source_target_pairs={{0,1},{1,0},{2,3},{3,2},{4,5},{5,4},{6,7},{7,6},{8,9},{9,8},{10,11... | collective-permute-start | bytes 1572872 | tf_op jit(solution)/shard_map/ppermute | solution.py:21
  66.7 26.2 %collective-permute-start.5 = (bf16[64,2048]{1,0:T(8,128)(2,1)S(1)}, bf16[64,2048]{1,0:T(8,128)(2,1)S(1)}, u32[]{:S(2)}, u32[]{:S(2)}) collective-permute-start(bf16[64,2048]{1,0:T(8,128)(2,1)S(1)} %slice.71), channel_id=1, source_target_pairs={{0,2},{1,3},{2,0},{3,1},{4,6},{5,7},{6,4},{7,5},{8,10},{9,11},{10,... | collective-permute-start | bytes 786440 | tf_op jit(solution)/shard_map/ppermute | solution.py:21
  69.6 12.2 %collective-permute-start.21 = (bf16[128,2048]{1,0:T(8,128)(2,1)S(1)}, bf16[128,2048]{1,0:T(8,128)(2,1)S(1)}, u32[]{:S(2)}, u32[]{:S(2)}) collective-permute-start(bf16[128,2048]{1,0:T(8,128)(2,1)S(1)} %get-tuple-element.30), channel_id=1, source_target_pairs={{0,1},{1,0},{2,3},{3,2},{4,5},{5,4},{6,7},{7,6},{8,9},{9,8},{10,11... | collective-permute-start | bytes 1572872 | tf_op jit(solution)/shard_map/ppermute | solution.py:21
  70.2 10.1 %collective-permute-start.10 = (bf16[64,2048]{1,0:T(8,128)(2,1)S(1)}, bf16[64,2048]{1,0:T(8,128)(2,1)S(1)}, u32[]{:S(2)}, u32[]{:S(2)}) collective-permute-start(bf16[64,2048]{1,0:T(8,128)(2,1)S(1)} %slice.70), channel_id=1, source_target_pairs={{0,2},{1,3},{2,0},{3,1},{4,6},{5,7},{6,4},{7,5},{8,10},{9,11},{10,... | collective-permute-start | bytes 786440 | tf_op jit(solution)/shard_map/ppermute | solution.py:21
  71.6 14.2 %collective-permute-start.16 = (bf16[64,2048]{1,0:T(8,128)(2,1)S(1)}, bf16[64,2048]{1,0:T(8,128)(2,1)S(1)}, u32[]{:S(2)}, u32[]{:S(2)}) collective-permute-start(bf16[64,2048]{1,0:T(8,128)(2,1)S(1)} %slice.69), channel_id=1, source_target_pairs={{0,2},{1,3},{2,0},{3,1},{4,6},{5,7},{6,4},{7,5},{8,10},{9,11},{10,... | collective-permute-start | bytes 786440 | tf_op jit(solution)/shard_map/ppermute | solution.py:21
  80.3 12.6 %collective-permute-start.11 = (bf16[64,2048]{1,0:T(8,128)(2,1)S(1)}, bf16[64,2048]{1,0:T(8,128)(2,1)S(1)}, u32[]{:S(2)}, u32[]{:S(2)}) collective-permute-start(bf16[64,2048]{1,0:T(8,128)(2,1)S(1)} %fusion.2), channel_id=1, source_target_pairs={{0,4},{1,5},{2,6},{3,7},{4,0},{5,1},{6,2},{7,3},{8,12},{9,13},{10,... | collective-permute-start | bytes 786440 | tf_op jit(solution)/shard_map/ppermute | solution.py:21
  82.0 9.5 %collective-permute-start.22 = (bf16[64,2048]{1,0:T(8,128)(2,1)S(1)}, bf16[64,2048]{1,0:T(8,128)(2,1)S(1)}, u32[]{:S(2)}, u32[]{:S(2)}) collective-permute-start(bf16[64,2048]{1,0:T(8,128)(2,1)S(1)} %slice.68), channel_id=1, source_target_pairs={{0,2},{1,3},{2,0},{3,1},{4,6},{5,7},{6,4},{7,5},{8,10},{9,11},{10,... | collective-permute-start | bytes 786440 | tf_op jit(solution)/shard_map/ppermute | solution.py:21
  85.9 19.5 %collective-permute-start.17 = (bf16[64,2048]{1,0:T(8,128)(2,1)S(1)}, bf16[64,2048]{1,0:T(8,128)(2,1)S(1)}, u32[]{:S(2)}, u32[]{:S(2)}) collective-permute-start(bf16[64,2048]{1,0:T(8,128)(2,1)S(1)} %fusion.1), channel_id=1, source_target_pairs={{0,8},{1,9},{2,10},{3,11},{4,12},{5,13},{6,14},{7,15},{8,0},{9,1},... | collective-permute-start | bytes 786440 | tf_op jit(solution)/shard_map/ppermute | solution.py:21
  91.5 20.6 %collective-permute-start.23 = (bf16[64,2048]{1,0:T(8,128)(2,1)S(1)}, bf16[64,2048]{1,0:T(8,128)(2,1)S(1)}, u32[]{:S(2)}, u32[]{:S(2)}) collective-permute-start(bf16[64,2048]{1,0:T(8,128)(2,1)S(1)} %fusion), channel_id=1, source_target_pairs={{0,12},{1,13},{2,14},{3,15},{4,8},{5,9},{6,10},{7,11},{8,4},{9,5},... | collective-permute-start | bytes 786440 | tf_op jit(solution)/shard_map/ppermute | solution.py:21

commit v2 on v1

--- a/solution.py
+++ b/solution.py
@@ -343,6 +343,11 @@
         mine, other = half[:masked_row_count], half[masked_row_count:].astype(jnp.bfloat16)
         other = exchanged(other, "wide", 2)
         mine = mine + other.astype(jnp.float32)
+        if k % 2 == 0 and k:
+            relayed = exchanged(mine.astype(jnp.bfloat16), "wide", 4).astype(jnp.float32)
+            continue
+        if k > 1:
+            mine = mine + relayed
         if k:
             mine = exchanged(mine.astype(jnp.bfloat16), "wide", 4 * k).astype(jnp.float32)
         total = total + mine

time: 113 us -> 106 us (0.938)
  waiting for transfers between devices: 55.8 us -> 48.9 us
    ppermute x24, waiting for transfers between devices: 55.8 us -> 48.9 us  [exchanged(): lax.ppermute(shard, axis, [(i, i ^ distance) for i in range(lax.axis_size...]
  transfers between devices with their start and end apart: 24 -> 24, of which waited for: 12 -> 11; matrix products, arithmetic and copies ran while one was open for 3% -> 3% of each run, Pallas kernels for 9% -> 10%
where the time goes in v2:
time: 106 us; the launch traced here: 105 us
  waiting for transfers between devices  48.9 us (46%)
  Pallas kernels  28.5 us (27%)
  starting transfers between devices  22.2 us (21%)
  other arithmetic  3.65 us (3%)
  local copies, waits for them, and re-layouts  1.54 us (1%)
    ppermute x24, waiting for transfers between devices, exchanged(): lax.ppermute(shard, axis, [(i, i ^ distance) for i in range(lax.axis_size...  48.9 us
    ppermute x24, starting transfers between devices, exchanged(): lax.ppermute(shard, axis, [(i, i ^ distance) for i in range(lax.axis_size...  22.2 us
    pallas_call x1, Pallas kernels, attend_cache(): pl.pallas_call(cache_kernel, grid=(KEY_VALUE_HEADS,), in_specs=[pl.BlockS...  17.3 us
    pallas_call x4, Pallas kernels, expert(): pl.pallas_call(functools.partial(expert_kernel, experts=experts), in_spec...  10.5 us
  transfers between devices with their start and end apart: 24, of which 11 were waited for; matrix products, arithmetic and copies ran while one was open for 3% of the time, Pallas kernels for 10%

profile of v2, /device:TPU:15, one launch (start us, length us, event | category | flops | bytes accessed | tf_op | source)
XLA Modules:
  0.0 105.0 jit_solution(1454321960167398667)
XLA Ops:
  0.0 0.7 collective-permute-start
  0.7 0.7 reduce_sum.18
  1.4 0.7 broadcast_divide_fusion
  2.1 0.7 select_reduce_fusion
  3.0 17.3 %cache_attention.1 = (f32[64,2048]{1,0:T(8,128)S(1)}, bf16[64,128]{1,0:T(8,128)(2,1)S(1)}, bf16[64,2176]{1,0:T(8,128)(2,1)S(1)}) custom-call(s32[1]{0:T(128)} %bitcast.device_ref, s32[8]{0:T(128)} %lengths_ref.1, s32[8,128]{1,0:T(8,128)} %positions_ref.1, bf16[64,2048]{1,0:T(8,128)(2,1)} %own_ref.1, bf16[64,2048]{1,0:T(8,128)(2,1)S(1)} %collective-permute-done.visit_ref, ...), custom_call_target="tpu_custom_call" | custom-call | tf_op jit(solution)/shard_map/cache_attention/pallas_call | solution.py:160
  20.6 1.4 %collective-permute-done.1.far_ref = bf16[64,2176]{1,0:T(8,128)(2,1)S(1)} collective-permute-done((bf16[64,2176]{1,0:T(8,128)(2,1)S(1)}, bf16[64,2176]{1,0:T(8,128)(2,1)S(1)}, u32[]{:S(2)}, u32[]{:S(2)}) %collective-permute-start.1) | collective-permute-done | bytes 278560 | tf_op jit(solution)/shard_map/ppermute | solution.py:21
  21.9 0.9 copy-done.3
  22.9 0.8 merge_norm.1
  23.7 0.2 collective-permute-start.6
  23.9 2.3 %collective-permute-start.12 = (bf16[64,2176]{1,0:T(8,128)(2,1)S(1)}, bf16[64,2176]{1,0:T(8,128)(2,1)S(1)}, u32[]{:S(2)}, u32[]{:S(2)}) collective-permute-start(bf16[64,2176]{1,0:T(8,128)(2,1)S(1)} %get-tuple-element.22), channel_id=1, source_target_pairs={{0,8},{1,9},{2,10},{3,11},{4,12},{5,13},{6,14},{7,15},{8,0},{9,1},... | collective-permute-start | bytes 835592 | tf_op jit(solution)/shard_map/ppermute | solution.py:21
  26.2 0.2 collective-permute-start.2
  26.5 7.3 %collective-permute-done.2 = bf16[64,2176]{1,0:T(8,128)(2,1)S(1)} collective-permute-done((bf16[64,2176]{1,0:T(8,128)(2,1)S(1)}, bf16[64,2176]{1,0:T(8,128)(2,1)S(1)}, u32[]{:S(2)}, u32[]{:S(2)}) %collective-permute-start.2) | collective-permute-done | bytes 278560 | tf_op jit(solution)/shard_map/ppermute | solution.py:21
  33.8 1.6 %collective-permute-start.3 = (bf16[128,2176]{1,0:T(8,128)(2,1)S(1)}, bf16[128,2176]{1,0:T(8,128)(2,1)S(1)}, u32[]{:S(2)}, u32[]{:S(2)}) collective-permute-start(bf16[128,2176]{1,0:T(8,128)(2,1)S(1)} %constant_dynamic-update-slice_fusion.near_ref), channel_id=1, source_target_pairs={{0,1},{1,0},{2,3},{3,2},{4,5},{5,4},{6,7},{7,6},{8,9},{9,8},{10,11... | collective-permute-start | bytes 1671176 | tf_op jit(solution)/shard_map/ppermute | solution.py:21
  35.4 0.3 collective-permute-done.6
  35.6 0.2 collective-permute-start.7
  35.9 3.0 %collective-permute-done.12 = bf16[64,2176]{1,0:T(8,128)(2,1)S(1)} collective-permute-done((bf16[64,2176]{1,0:T(8,128)(2,1)S(1)}, bf16[64,2176]{1,0:T(8,128)(2,1)S(1)}, u32[]{:S(2)}, u32[]{:S(2)}) %collective-permute-start.12) | collective-permute-done | bytes 278560 | tf_op jit(solution)/shard_map/ppermute | solution.py:21
  38.9 0.2 collective-permute-start.14
  39.1 0.3 collective-permute-start.13
  39.4 3.4 %collective-permute-done.7 = bf16[64,2176]{1,0:T(8,128)(2,1)S(1)} collective-permute-done((bf16[64,2176]{1,0:T(8,128)(2,1)S(1)}, bf16[64,2176]{1,0:T(8,128)(2,1)S(1)}, u32[]{:S(2)}, u32[]{:S(2)}) %collective-permute-start.7) | collective-permute-done | bytes 278560 | tf_op jit(solution)/shard_map/ppermute | solution.py:21
  42.9 3.4 %collective-permute-start.8 = (bf16[128,2176]{1,0:T(8,128)(2,1)S(1)}, bf16[128,2176]{1,0:T(8,128)(2,1)S(1)}, u32[]{:S(2)}, u32[]{:S(2)}) collective-permute-start(bf16[128,2176]{1,0:T(8,128)(2,1)S(1)} %constant_dynamic-update-slice_fusion.2.near_ref), channel_id=1, source_target_pairs={{0,1},{1,0},{2,3},{3,2},{4,5},{5,4},{6,7},{7,6},{8,9},{9,8},{10,11... | collective-permute-start | bytes 1671176 | tf_op jit(solution)/shard_map/ppermute | solution.py:21
  46.3 2.6 %collective-permute-done.14 = bf16[64,2176]{1,0:T(8,128)(2,1)S(1)} collective-permute-done((bf16[64,2176]{1,0:T(8,128)(2,1)S(1)}, bf16[64,2176]{1,0:T(8,128)(2,1)S(1)}, u32[]{:S(2)}, u32[]{:S(2)}) %collective-permute-start.14) | collective-permute-done | bytes 278560 | tf_op jit(solution)/shard_map/ppermute | solution.py:21
  48.9 1.9 %collective-permute-start.19 = (bf16[128,2176]{1,0:T(8,128)(2,1)S(1)}, bf16[128,2176]{1,0:T(8,128)(2,1)S(1)}, u32[]{:S(2)}, u32[]{:S(2)}) collective-permute-start(bf16[128,2176]{1,0:T(8,128)(2,1)S(1)} %constant_dynamic-update-slice_fusion.6.near_ref), channel_id=1, source_target_pairs={{0,1},{1,0},{2,3},{3,2},{4,5},{5,4},{6,7},{7,6},{8,9},{9,8},{10,11... | collective-permute-start | bytes 1671176 | tf_op jit(solution)/shard_map/ppermute | solution.py:21
  50.8 2.2 %collective-permute-start.15 = (bf16[64,2176]{1,0:T(8,128)(2,1)S(1)}, bf16[64,2176]{1,0:T(8,128)(2,1)S(1)}, u32[]{:S(2)}, u32[]{:S(2)}) collective-permute-start(bf16[64,2176]{1,0:T(8,128)(2,1)S(1)} %collective-permute-done.14), channel_id=1, source_target_pairs={{0,4},{1,5},{2,6},{3,7},{4,0},{5,1},{6,2},{7,3},{8,12},{9,13},{10,... | collective-permute-start | bytes 835592 | tf_op jit(solution)/shard_map/ppermute | solution.py:21
  53.0 2.6 %expert.4 = (f32[128,2048]{1,0:T(8,128)S(1)}, bf16[128,2048]{1,0:T(8,128)(2,1)S(1)}) custom-call(s32[1]{0:T(128)} %bitcast.device_ref, bf16[128,2176]{1,0:T(8,128)(2,1)S(1)} %constant_dynamic-update-slice_fusion.near_ref, bf16[128,2176]{1,0:T(8,128)(2,1)S(1)} %collective-permute-done.3.far_ref, bf16[1,2048,768]{2,1,0:T(8,128)(2,1)S(1)} %copy-done, ...), custom_call_target="tpu_custom_call" | custom-call | tf_op jit(solution)/shard_map/expert/pallas_call | solution.py:279
  55.6 0.4 collective-permute-start.4
  56.1 3.9 %collective-permute-done.15 = bf16[64,2176]{1,0:T(8,128)(2,1)S(1)} collective-permute-done((bf16[64,2176]{1,0:T(8,128)(2,1)S(1)}, bf16[64,2176]{1,0:T(8,128)(2,1)S(1)}, u32[]{:S(2)}, u32[]{:S(2)}) %collective-permute-start.15) | collective-permute-done | bytes 278560 | tf_op jit(solution)/shard_map/ppermute | solution.py:21
  60.0 0.7 collective-permute-start.16
  60.7 2.6 %expert.7 = (f32[128,2048]{1,0:T(8,128)S(1)}, bf16[128,2048]{1,0:T(8,128)(2,1)S(1)}) custom-call(s32[1]{0:T(128)} %bitcast.device_ref, bf16[128,2176]{1,0:T(8,128)(2,1)S(1)} %constant_dynamic-update-slice_fusion.6.near_ref, bf16[128,2176]{1,0:T(8,128)(2,1)S(1)} %collective-permute-done.19.far_ref, bf16[1,2048,768]{2,1,0:T(8,128)(2,1)S(1)} %copy-done, ...), custom_call_target="tpu_custom_call" | custom-call | tf_op jit(solution)/shard_map/expert/pallas_call | solution.py:279
  63.4 2.6 %expert.5 = (f32[128,2048]{1,0:T(8,128)S(1)}, bf16[128,2048]{1,0:T(8,128)(2,1)S(1)}) custom-call(s32[1]{0:T(128)} %bitcast.device_ref, bf16[128,2176]{1,0:T(8,128)(2,1)S(1)} %constant_dynamic-update-slice_fusion.2.near_ref, bf16[128,2176]{1,0:T(8,128)(2,1)S(1)} %collective-permute-done.8.far_ref, bf16[1,2048,768]{2,1,0:T(8,128)(2,1)S(1)} %copy-done, ...), custom_call_target="tpu_custom_call" | custom-call | tf_op jit(solution)/shard_map/expert/pallas_call | solution.py:279
  66.0 0.6 collective-permute-start.9
  66.6 0.1 convert_add_fusion.3
  66.7 0.3 collective-permute-start.5
  67.0 2.6 %expert.6 = (f32[128,2048]{1,0:T(8,128)S(1)}, bf16[128,2048]{1,0:T(8,128)(2,1)S(1)}) custom-call(s32[1]{0:T(128)} %bitcast.device_ref, bf16[128,2176]{1,0:T(8,128)(2,1)S(1)} %constant_dynamic-update-slice_fusion.4.near_ref, bf16[128,2176]{1,0:T(8,128)(2,1)S(1)} %collective-permute-done.16.far_ref, bf16[1,2048,768]{2,1,0:T(8,128)(2,1)S(1)} %copy-done, ...), custom_call_target="tpu_custom_call" | custom-call | tf_op jit(solution)/shard_map/expert/pallas_call | solution.py:279
  69.6 0.4 collective-permute-start.17
  70.0 0.1 convert_add_fusion
  70.2 1.3 %collective-permute-start.21 = (bf16[64,2048]{1,0:T(8,128)(2,1)S(1)}, bf16[64,2048]{1,0:T(8,128)(2,1)S(1)}, u32[]{:S(2)}, u32[]{:S(2)}) collective-permute-start(bf16[64,2048]{1,0:T(8,128)(2,1)S(1)} %slice.68), channel_id=1, source_target_pairs={{0,2},{1,3},{2,0},{3,1},{4,6},{5,7},{6,4},{7,5},{8,10},{9,11},{10,... | collective-permute-start | bytes 786440 | tf_op jit(solution)/shard_map/ppermute | solution.py:21
  71.5 0.1 convert_add_fusion.2
  71.6 0.3 collective-permute-start.10
  71.9 8.3 %collective-permute-done.21 = bf16[64,2048]{1,0:T(8,128)(2,1)S(1)} collective-permute-done((bf16[64,2048]{1,0:T(8,128)(2,1)S(1)}, bf16[64,2048]{1,0:T(8,128)(2,1)S(1)}, u32[]{:S(2)}, u32[]{:S(2)}) %collective-permute-start.21) | collective-permute-done | bytes 262176 | tf_op jit(solution)/shard_map/ppermute | solution.py:21
  80.3 1.5 %collective-permute-start.22 = (bf16[64,2048]{1,0:T(8,128)(2,1)S(1)}, bf16[64,2048]{1,0:T(8,128)(2,1)S(1)}, u32[]{:S(2)}, u32[]{:S(2)}) collective-permute-start(bf16[64,2048]{1,0:T(8,128)(2,1)S(1)} %fusion), channel_id=1, source_target_pairs={{0,4},{1,5},{2,6},{3,7},{4,0},{5,1},{6,2},{7,3},{8,12},{9,13},{10,... | collective-permute-start | bytes 786440 | tf_op jit(solution)/shard_map/ppermute | solution.py:21
  81.8 0.1 convert_add_fusion.1
  82.0 0.3 collective-permute-start.18
  82.3 3.6 %collective-permute-done.10 = bf16[64,2048]{1,0:T(8,128)(2,1)S(1)} collective-permute-done((bf16[64,2048]{1,0:T(8,128)(2,1)S(1)}, bf16[64,2048]{1,0:T(8,128)(2,1)S(1)}, u32[]{:S(2)}, u32[]{:S(2)}) %collective-permute-start.10) | collective-permute-done | bytes 262176 | tf_op jit(solution)/shard_map/ppermute | solution.py:21
  85.9 1.5 %collective-permute-start.11 = (bf16[64,2048]{1,0:T(8,128)(2,1)S(1)}, bf16[64,2048]{1,0:T(8,128)(2,1)S(1)}, u32[]{:S(2)}, u32[]{:S(2)}) collective-permute-start(bf16[64,2048]{1,0:T(8,128)(2,1)S(1)} %fusion.3), channel_id=1, source_target_pairs={{0,4},{1,5},{2,6},{3,7},{4,0},{5,1},{6,2},{7,3},{8,12},{9,13},{10,... | collective-permute-start | bytes 786440 | tf_op jit(solution)/shard_map/ppermute | solution.py:21
  87.5 4.0 %collective-permute-done.18 = bf16[64,2048]{1,0:T(8,128)(2,1)S(1)} collective-permute-done((bf16[64,2048]{1,0:T(8,128)(2,1)S(1)}, bf16[64,2048]{1,0:T(8,128)(2,1)S(1)}, u32[]{:S(2)}, u32[]{:S(2)}) %collective-permute-start.18) | collective-permute-done | bytes 262176 | tf_op jit(solution)/shard_map/ppermute | solution.py:21
  91.6 1.4 %collective-permute-start.23 = (bf16[64,2048]{1,0:T(8,128)(2,1)S(1)}, bf16[64,2048]{1,0:T(8,128)(2,1)S(1)}, u32[]{:S(2)}, u32[]{:S(2)}) collective-permute-start(bf16[64,2048]{1,0:T(8,128)(2,1)S(1)} %fusion.2), channel_id=1, source_target_pairs={{0,12},{1,13},{2,14},{3,15},{4,8},{5,9},{6,10},{7,11},{8,4},{9,5},... | collective-permute-start | bytes 786440 | tf_op jit(solution)/shard_map/ppermute | solution.py:21
  92.9 11.3 %collective-permute-done.23 = bf16[64,2048]{1,0:T(8,128)(2,1)S(1)} collective-permute-done((bf16[64,2048]{1,0:T(8,128)(2,1)S(1)}, bf16[64,2048]{1,0:T(8,128)(2,1)S(1)}, u32[]{:S(2)}, u32[]{:S(2)}) %collective-permute-start.23) | collective-permute-done | bytes 262176 | tf_op jit(solution)/shard_map/ppermute | solution.py:21
  104.2 0.8 fusion.7
  (46 shorter events, 1.1 us)
Async XLA Ops:
  0.0 21.9 %copy-start.4 = (f32[2048]{0:T(1024)S(1)}, f32[2048]{0:T(1024)}, u32[]{:S(2)}) copy-start(f32[2048]{0:T(1024)} %param.16) | copy-start | bytes 24580
  0.0 3.0 %collective-permute-start = (bf16[64,2048]{1,0:T(8,128)(2,1)}, bf16[64,2048]{1,0:T(8,128)(2,1)S(1)}, u32[]{:S(2)}, u32[]{:S(2)}) collective-permute-start(bf16[64,2048]{1,0:T(8,128)(2,1)} %own_ref.1), channel_id=1, source_target_pairs={{0,1},{1,0},{2,3},{3,2},{4,5},{5,4},{6,7},{7,6},{8,9},{9,8},{10,11... | collective-permute-start | bytes 786440 | tf_op jit(solution)/shard_map/ppermute | solution.py:21
  2.9 50.1 %copy-start.2 = (bf16[1,768,2048]{2,1,0:T(8,128)(2,1)S(1)}, bf16[1,768,2048]{2,1,0:T(8,128)(2,1)}, u32[]{:S(2)}) copy-start(bf16[1,768,2048]{2,1,0:T(8,128)(2,1)} %down_ref.7) | copy-start | bytes 9437188
  3.0 50.0 %copy-start.1 = (bf16[1,2048,768]{2,1,0:T(8,128)(2,1)S(1)}, bf16[1,2048,768]{2,1,0:T(8,128)(2,1)}, u32[]{:S(2)}) copy-start(bf16[1,2048,768]{2,1,0:T(8,128)(2,1)} %up_ref.7) | copy-start | bytes 9437188
  20.3 32.7 %copy-start = (bf16[1,2048,768]{2,1,0:T(8,128)(2,1)S(1)}, bf16[1,2048,768]{2,1,0:T(8,128)(2,1)}, u32[]{:S(2)}) copy-start(bf16[1,2048,768]{2,1,0:T(8,128)(2,1)} %gate_ref.7) | copy-start | bytes 9437188
  20.3 1.6 %collective-permute-start.1 = (bf16[64,2176]{1,0:T(8,128)(2,1)S(1)}, bf16[64,2176]{1,0:T(8,128)(2,1)S(1)}, u32[]{:S(2)}, u32[]{:S(2)}) collective-permute-start(bf16[64,2176]{1,0:T(8,128)(2,1)S(1)} %get-tuple-element.20), channel_id=1, source_target_pairs={{0,1},{1,0},{2,3},{3,2},{4,5},{5,4},{6,7},{7,6},{8,9},{9,8},{10,11... | collective-permute-start | bytes 835592 | tf_op jit(solution)/shard_map/ppermute | solution.py:21
  21.9 1.0 copy-start.3
  23.7 12.0 %collective-permute-start.6 = (bf16[64,2176]{1,0:T(8,128)(2,1)S(1)}, bf16[64,2176]{1,0:T(8,128)(2,1)S(1)}, u32[]{:S(2)}, u32[]{:S(2)}) collective-permute-start(bf16[64,2176]{1,0:T(8,128)(2,1)S(1)} %get-tuple-element.22), channel_id=1, source_target_pairs={{0,4},{1,5},{2,6},{3,7},{4,0},{5,1},{6,2},{7,3},{8,12},{9,13},{10,... | collective-permute-start | bytes 835592 | tf_op jit(solution)/shard_map/ppermute | solution.py:21
  23.9 14.9 %collective-permute-start.12 = (bf16[64,2176]{1,0:T(8,128)(2,1)S(1)}, bf16[64,2176]{1,0:T(8,128)(2,1)S(1)}, u32[]{:S(2)}, u32[]{:S(2)}) collective-permute-start(bf16[64,2176]{1,0:T(8,128)(2,1)S(1)} %get-tuple-element.22), channel_id=1, source_target_pairs={{0,8},{1,9},{2,10},{3,11},{4,12},{5,13},{6,14},{7,15},{8,0},{9,1},... | collective-permute-start | bytes 835592 | tf_op jit(solution)/shard_map/ppermute | solution.py:21
  26.2 7.5 %collective-permute-start.2 = (bf16[64,2176]{1,0:T(8,128)(2,1)S(1)}, bf16[64,2176]{1,0:T(8,128)(2,1)S(1)}, u32[]{:S(2)}, u32[]{:S(2)}) collective-permute-start(bf16[64,2176]{1,0:T(8,128)(2,1)S(1)} %get-tuple-element.22), channel_id=1, source_target_pairs={{0,2},{1,3},{2,0},{3,1},{4,6},{5,7},{6,4},{7,5},{8,10},{9,11},{10,... | collective-permute-start | bytes 835592 | tf_op jit(solution)/shard_map/ppermute | solution.py:21
  33.8 19.2 %collective-permute-start.3 = (bf16[128,2176]{1,0:T(8,128)(2,1)S(1)}, bf16[128,2176]{1,0:T(8,128)(2,1)S(1)}, u32[]{:S(2)}, u32[]{:S(2)}) collective-permute-start(bf16[128,2176]{1,0:T(8,128)(2,1)S(1)} %constant_dynamic-update-slice_fusion.near_ref), channel_id=1, source_target_pairs={{0,1},{1,0},{2,3},{3,2},{4,5},{5,4},{6,7},{7,6},{8,9},{9,8},{10,11... | collective-permute-start | bytes 1671176 | tf_op jit(solution)/shard_map/ppermute | solution.py:21
  35.6 7.2 %collective-permute-start.7 = (bf16[64,2176]{1,0:T(8,128)(2,1)S(1)}, bf16[64,2176]{1,0:T(8,128)(2,1)S(1)}, u32[]{:S(2)}, u32[]{:S(2)}) collective-permute-start(bf16[64,2176]{1,0:T(8,128)(2,1)S(1)} %collective-permute-done.6), channel_id=1, source_target_pairs={{0,2},{1,3},{2,0},{3,1},{4,6},{5,7},{6,4},{7,5},{8,10},{9,11},{10,... | collective-permute-start | bytes 835592 | tf_op jit(solution)/shard_map/ppermute | solution.py:21
  38.9 10.0 %collective-permute-start.14 = (bf16[64,2176]{1,0:T(8,128)(2,1)S(1)}, bf16[64,2176]{1,0:T(8,128)(2,1)S(1)}, u32[]{:S(2)}, u32[]{:S(2)}) collective-permute-start(bf16[64,2176]{1,0:T(8,128)(2,1)S(1)} %collective-permute-done.12), channel_id=1, source_target_pairs={{0,2},{1,3},{2,0},{3,1},{4,6},{5,7},{6,4},{7,5},{8,10},{9,11},{10,... | collective-permute-start | bytes 835592 | tf_op jit(solution)/shard_map/ppermute | solution.py:21
  39.1 17.0 %collective-permute-start.13 = (bf16[64,2176]{1,0:T(8,128)(2,1)S(1)}, bf16[64,2176]{1,0:T(8,128)(2,1)S(1)}, u32[]{:S(2)}, u32[]{:S(2)}) collective-permute-start(bf16[64,2176]{1,0:T(8,128)(2,1)S(1)} %collective-permute-done.12), channel_id=1, source_target_pairs={{0,4},{1,5},{2,6},{3,7},{4,0},{5,1},{6,2},{7,3},{8,12},{9,13},{10,... | collective-permute-start | bytes 835592 | tf_op jit(solution)/shard_map/ppermute | solution.py:21
  42.9 20.5 %collective-permute-start.8 = (bf16[128,2176]{1,0:T(8,128)(2,1)S(1)}, bf16[128,2176]{1,0:T(8,128)(2,1)S(1)}, u32[]{:S(2)}, u32[]{:S(2)}) collective-permute-start(bf16[128,2176]{1,0:T(8,128)(2,1)S(1)} %constant_dynamic-update-slice_fusion.2.near_ref), channel_id=1, source_target_pairs={{0,1},{1,0},{2,3},{3,2},{4,5},{5,4},{6,7},{7,6},{8,9},{9,8},{10,11... | collective-permute-start | bytes 1671176 | tf_op jit(solution)/shard_map/ppermute | solution.py:21
  48.9 11.8 %collective-permute-start.19 = (bf16[128,2176]{1,0:T(8,128)(2,1)S(1)}, bf16[128,2176]{1,0:T(8,128)(2,1)S(1)}, u32[]{:S(2)}, u32[]{:S(2)}) collective-permute-start(bf16[128,2176]{1,0:T(8,128)(2,1)S(1)} %constant_dynamic-update-slice_fusion.6.near_ref), channel_id=1, source_target_pairs={{0,1},{1,0},{2,3},{3,2},{4,5},{5,4},{6,7},{7,6},{8,9},{9,8},{10,11... | collective-permute-start | bytes 1671176 | tf_op jit(solution)/shard_map/ppermute | solution.py:21
  50.8 9.2 %collective-permute-start.15 = (bf16[64,2176]{1,0:T(8,128)(2,1)S(1)}, bf16[64,2176]{1,0:T(8,128)(2,1)S(1)}, u32[]{:S(2)}, u32[]{:S(2)}) collective-permute-start(bf16[64,2176]{1,0:T(8,128)(2,1)S(1)} %collective-permute-done.14), channel_id=1, source_target_pairs={{0,4},{1,5},{2,6},{3,7},{4,0},{5,1},{6,2},{7,3},{8,12},{9,13},{10,... | collective-permute-start | bytes 835592 | tf_op jit(solution)/shard_map/ppermute | solution.py:21
  55.6 10.9 %collective-permute-start.4 = (bf16[128,2048]{1,0:T(8,128)(2,1)S(1)}, bf16[128,2048]{1,0:T(8,128)(2,1)S(1)}, u32[]{:S(2)}, u32[]{:S(2)}) collective-permute-start(bf16[128,2048]{1,0:T(8,128)(2,1)S(1)} %get-tuple-element.24), channel_id=1, source_target_pairs={{0,1},{1,0},{2,3},{3,2},{4,5},{5,4},{6,7},{7,6},{8,9},{9,8},{10,11... | collective-permute-start | bytes 1572872 | tf_op jit(solution)/shard_map/ppermute | solution.py:21
  60.0 7.1 %collective-permute-start.16 = (bf16[128,2176]{1,0:T(8,128)(2,1)S(1)}, bf16[128,2176]{1,0:T(8,128)(2,1)S(1)}, u32[]{:S(2)}, u32[]{:S(2)}) collective-permute-start(bf16[128,2176]{1,0:T(8,128)(2,1)S(1)} %constant_dynamic-update-slice_fusion.4.near_ref), channel_id=1, source_target_pairs={{0,1},{1,0},{2,3},{3,2},{4,5},{5,4},{6,7},{7,6},{8,9},{9,8},{10,11... | collective-permute-start | bytes 1671176 | tf_op jit(solution)/shard_map/ppermute | solution.py:21
  63.3 6.7 %collective-permute-start.20 = (bf16[128,2048]{1,0:T(8,128)(2,1)S(1)}, bf16[128,2048]{1,0:T(8,128)(2,1)S(1)}, u32[]{:S(2)}, u32[]{:S(2)}) collective-permute-start(bf16[128,2048]{1,0:T(8,128)(2,1)S(1)} %get-tuple-element.30), channel_id=1, source_target_pairs={{0,1},{1,0},{2,3},{3,2},{4,5},{5,4},{6,7},{7,6},{8,9},{9,8},{10,11... | collective-permute-start | bytes 1572872 | tf_op jit(solution)/shard_map/ppermute | solution.py:21
  66.0 5.5 %collective-permute-start.9 = (bf16[128,2048]{1,0:T(8,128)(2,1)S(1)}, bf16[128,2048]{1,0:T(8,128)(2,1)S(1)}, u32[]{:S(2)}, u32[]{:S(2)}) collective-permute-start(bf16[128,2048]{1,0:T(8,128)(2,1)S(1)} %get-tuple-element.26), channel_id=1, source_target_pairs={{0,1},{1,0},{2,3},{3,2},{4,5},{5,4},{6,7},{7,6},{8,9},{9,8},{10,11... | collective-permute-start | bytes 1572872 | tf_op jit(solution)/shard_map/ppermute | solution.py:21
  66.7 26.2 %collective-permute-start.5 = (bf16[64,2048]{1,0:T(8,128)(2,1)S(1)}, bf16[64,2048]{1,0:T(8,128)(2,1)S(1)}, u32[]{:S(2)}, u32[]{:S(2)}) collective-permute-start(bf16[64,2048]{1,0:T(8,128)(2,1)S(1)} %slice.71), channel_id=1, source_target_pairs={{0,2},{1,3},{2,0},{3,1},{4,6},{5,7},{6,4},{7,5},{8,10},{9,11},{10,... | collective-permute-start | bytes 786440 | tf_op jit(solution)/shard_map/ppermute | solution.py:21
  69.6 12.2 %collective-permute-start.17 = (bf16[128,2048]{1,0:T(8,128)(2,1)S(1)}, bf16[128,2048]{1,0:T(8,128)(2,1)S(1)}, u32[]{:S(2)}, u32[]{:S(2)}) collective-permute-start(bf16[128,2048]{1,0:T(8,128)(2,1)S(1)} %get-tuple-element.28), channel_id=1, source_target_pairs={{0,1},{1,0},{2,3},{3,2},{4,5},{5,4},{6,7},{7,6},{8,9},{9,8},{10,11... | collective-permute-start | bytes 1572872 | tf_op jit(solution)/shard_map/ppermute | solution.py:21
  70.2 10.1 %collective-permute-start.21 = (bf16[64,2048]{1,0:T(8,128)(2,1)S(1)}, bf16[64,2048]{1,0:T(8,128)(2,1)S(1)}, u32[]{:S(2)}, u32[]{:S(2)}) collective-permute-start(bf16[64,2048]{1,0:T(8,128)(2,1)S(1)} %slice.68), channel_id=1, source_target_pairs={{0,2},{1,3},{2,0},{3,1},{4,6},{5,7},{6,4},{7,5},{8,10},{9,11},{10,... | collective-permute-start | bytes 786440 | tf_op jit(solution)/shard_map/ppermute | solution.py:21
  71.6 14.2 %collective-permute-start.10 = (bf16[64,2048]{1,0:T(8,128)(2,1)S(1)}, bf16[64,2048]{1,0:T(8,128)(2,1)S(1)}, u32[]{:S(2)}, u32[]{:S(2)}) collective-permute-start(bf16[64,2048]{1,0:T(8,128)(2,1)S(1)} %slice.70), channel_id=1, source_target_pairs={{0,2},{1,3},{2,0},{3,1},{4,6},{5,7},{6,4},{7,5},{8,10},{9,11},{10,... | collective-permute-start | bytes 786440 | tf_op jit(solution)/shard_map/ppermute | solution.py:21
  80.3 7.2 %collective-permute-start.22 = (bf16[64,2048]{1,0:T(8,128)(2,1)S(1)}, bf16[64,2048]{1,0:T(8,128)(2,1)S(1)}, u32[]{:S(2)}, u32[]{:S(2)}) collective-permute-start(bf16[64,2048]{1,0:T(8,128)(2,1)S(1)} %fusion), channel_id=1, source_target_pairs={{0,4},{1,5},{2,6},{3,7},{4,0},{5,1},{6,2},{7,3},{8,12},{9,13},{10,... | collective-permute-start | bytes 786440 | tf_op jit(solution)/shard_map/ppermute | solution.py:21
  82.0 9.5 %collective-permute-start.18 = (bf16[64,2048]{1,0:T(8,128)(2,1)S(1)}, bf16[64,2048]{1,0:T(8,128)(2,1)S(1)}, u32[]{:S(2)}, u32[]{:S(2)}) collective-permute-start(bf16[64,2048]{1,0:T(8,128)(2,1)S(1)} %slice.69), channel_id=1, source_target_pairs={{0,2},{1,3},{2,0},{3,1},{4,6},{5,7},{6,4},{7,5},{8,10},{9,11},{10,... | collective-permute-start | bytes 786440 | tf_op jit(solution)/shard_map/ppermute | solution.py:21
  85.9 7.0 %collective-permute-start.11 = (bf16[64,2048]{1,0:T(8,128)(2,1)S(1)}, bf16[64,2048]{1,0:T(8,128)(2,1)S(1)}, u32[]{:S(2)}, u32[]{:S(2)}) collective-permute-start(bf16[64,2048]{1,0:T(8,128)(2,1)S(1)} %fusion.3), channel_id=1, source_target_pairs={{0,4},{1,5},{2,6},{3,7},{4,0},{5,1},{6,2},{7,3},{8,12},{9,13},{10,... | collective-permute-start | bytes 786440 | tf_op jit(solution)/shard_map/ppermute | solution.py:21
  91.6 12.6 %collective-permute-start.23 = (bf16[64,2048]{1,0:T(8,128)(2,1)S(1)}, bf16[64,2048]{1,0:T(8,128)(2,1)S(1)}, u32[]{:S(2)}, u32[]{:S(2)}) collective-permute-start(bf16[64,2048]{1,0:T(8,128)(2,1)S(1)} %fusion.2), channel_id=1, source_target_pairs={{0,12},{1,13},{2,14},{3,15},{4,8},{5,9},{6,10},{7,11},{8,4},{9,5},... | collective-permute-start | bytes 786440 | tf_op jit(solution)/shard_map/ppermute | solution.py:21
